TPU v7x, 32 devices: a whole 2x2x4 slice. The times are simulated.
32 devices in a mesh: parts: 2 (over y), seq: 4 (over z), chan: 2 (over x), sub: 2 (over core).
Axes of the slice: x: 2, y: 2, z: 4, core: 2. Of those that a mesh axis runs over, the one named last changes fastest.
Arguments:
- signal: float32 [16, 16384], P(('parts', 'chan', 'sub'), 'seq'), parts along dimension 0, may hold values from -1 to 1
- filter_taps: float32 [16, 16384], P(('parts', 'chan', 'sub'), 'seq'), parts along dimension 0, may hold values from -4 to 4
- grad_out: float32 [16, 16384], P(('parts', 'chan', 'sub'), 'seq'), parts along dimension 0, may hold values from -6 to 6
- skip: float32 [16], P(('parts', 'chan', 'sub')), parts along dimension 0, may hold values from -4 to 4
Outputs:
- grad_signal: float32 [16, 16384], P(('parts', 'chan', 'sub'), 'seq'), parts along dimension 0
- grad_filter: float32 [16, 16384], P(('parts', 'chan', 'sub'), 'seq'), parts along dimension 0
- grad_skip: float32 [16], P(('parts', 'chan', 'sub')), parts along dimension 0
There are 2 independent parts, one for each index of `parts`. A program takes and returns all parts, laid end to end along the dimension named above; each array names one. Nothing has to cross between parts.
All inputs are finite; a program needn't handle non-finite values.
Results may differ from a plain program's by a relative error of at most 0.00013.
Values sent between devices are 32-bit elements; how exact they have to be, the bound alone decides.
No kernel may reach another device: no remote copies, remote signals or barrier semaphores. Data moves between devices by JAX's collectives and lax.ppermute only.
A program may use at most 64 MiB of HBM per device.

v0:
```python
import functools
import math

import jax
import jax.numpy as jnp
import ml_dtypes
import numpy as np
from jax import lax
from jax.experimental import pallas as pl
from jax.experimental.pallas import tpu as pltpu
from jax.sharding import PartitionSpec as P

LANES = 128
highest = lax.Precision.HIGHEST


def split_table(table):
    high = table.astype(np.float32).astype(ml_dtypes.bfloat16)
    low = (table - high.astype(np.float64)).astype(np.float32).astype(ml_dtypes.bfloat16)
    return high, low


def gathered_tables(length, groups):
    rows = length // LANES
    coarse = np.arange(rows, dtype=np.float64)
    fine = np.arange(LANES, dtype=np.float64)
    phase = 2.0 * np.pi / rows * (coarse[:, None] + 0.25) * coarse[None, :]
    first = np.concatenate([np.cos(phase), -np.sin(phase)])
    high, low = (part.reshape(2 * rows, groups, -1) for part in split_table(first))
    stage_first = np.concatenate([high, high, low, low], axis=2).reshape(2 * rows, 4 * rows)
    last = (first.T / length).reshape(groups, rows // groups, 2 * rows)
    turn = 2.0 * np.pi / length * (coarse[:, None] + 0.25) * fine[None, :]
    twiddle = np.stack([np.cos(turn), np.sin(turn)]).astype(np.float32)
    angle = 2.0 * np.pi / LANES * fine[:, None] * fine[None, :]
    cos, sin = np.cos(angle), np.sin(angle)
    second = np.block([[cos, -sin], [sin, cos]])
    return stage_first, twiddle, np.stack(split_table(second)), np.stack(split_table(last), axis=1)


def split(value):
    high = value.astype(jnp.bfloat16)
    return high, (value - high.astype(jnp.float32)).astype(jnp.bfloat16)


def dot(left, right):
    return jnp.dot(left, right, preferred_element_type=jnp.float32)


def product(left, right):
    return dot(left[0], right[0]) + dot(left[0], right[1]) + dot(left[1], right[0])


def stage_rows(block, channels):
    cells = block.shape[0] // 3
    pieces = []
    for channel in range(channels):
        for array in range(3):
            pieces.append(block[pl.ds(array * cells + channel, cells // channels, stride=channels)])
    value = jnp.concatenate(pieces, axis=1)
    high, low = split(value)
    return jnp.concatenate([high, low, high, low])


def stage_columns(table, group):
    width = table.shape[1] // lax.axis_size("seq")
    return table[:, pl.ds(pl.multiple_of(group * width, width), width)]


def own_kernel(channels, block, first, twiddle, second, last, out_ref):
    out_ref[...] = dot(stage_columns(first, lax.axis_index("seq")), stage_rows(block, channels))


def gathered_kernel(groups, channels, skip_ref, coarse_ref, *refs):
    blocks = refs[:groups]
    first, twiddle, second, last = refs[groups : groups + 4]
    grad_signal_ref, grad_filter_ref, grad_skip_ref = refs[groups + 4 :]
    device = lax.axis_index("seq")
    rows = twiddle.shape[1]
    height = rows // groups

    columns = [stage_columns(first, lax.bitwise_xor(device, step)) for step in range(1, groups)]
    data = [stage_rows(block, channels) for block in blocks[1:]]
    coarse = coarse_ref[...] + dot(jnp.concatenate(columns, axis=1), jnp.concatenate(data))
    cos, sin = twiddle[0], twiddle[1]
    turned = []
    for index in range(3 * channels):
        lanes = slice(index * LANES, (index + 1) * LANES)
        real, imag = coarse[:rows, lanes], coarse[rows:, lanes]
        turned.append(jnp.concatenate([real * cos + imag * sin, imag * cos - real * sin], axis=1))
    spectra = product(split(jnp.concatenate(turned)), (second[0], second[1]))
    products = []
    for channel in range(channels):
        grad = spectra[(3 * channel + 2) * rows : (3 * channel + 3) * rows]
        grad_real, grad_imag = grad[:, :LANES], grad[:, LANES:]
        for array in range(2):
            other = spectra[(3 * channel + array) * rows : (3 * channel + array + 1) * rows]
            real, imag = other[:, :LANES], other[:, LANES:]
            products.append(
                jnp.concatenate([real * grad_real + imag * grad_imag, imag * grad_real - real * grad_imag], axis=1)
            )
    back = product(split(jnp.concatenate(products)), (second[0], second[1]))
    spread = []
    for index in range(2 * channels):
        value = back[index * rows : (index + 1) * rows]
        real, minus = value[:, :LANES], value[:, LANES:]
        spread.append(jnp.concatenate([real * cos + minus * sin, real * sin - minus * cos]))
    result = product((last[device, 0], last[device, 1]), split(jnp.concatenate(spread, axis=1)))

    cells = height * channels
    total = sum(block[cells : 2 * cells] * block[2 * cells :] for block in blocks)
    owner = lax.broadcasted_iota(jnp.int32, total.shape, 0) % channels
    for channel in range(channels):
        grad_skip_ref[channel] = jnp.sum(jnp.where(owner == channel, total, 0.0))
        mine = pl.ds(channel, height, stride=channels)
        lanes = 2 * channel * LANES
        kept = skip_ref[channel] * blocks[0][pl.ds(2 * cells + channel, height, stride=channels)]
        grad_signal_ref[mine, :] = result[:, lanes : lanes + LANES] + kept
        grad_filter_ref[mine, :] = result[:, lanes + LANES : lanes + 2 * LANES]


def dense(value):
    channels, cells = value.shape
    return value.reshape(channels, cells // LANES, LANES).transpose(1, 0, 2).reshape(-1, LANES)


def undense(value, channels):
    return value.reshape(-1, channels, LANES).transpose(1, 0, 2).reshape(channels, -1)


def gathered_body(signal, filter_taps, grad_out, skip):
    groups = lax.axis_size("seq")
    channels, cells = signal.shape
    length = cells * groups
    rows = length // LANES
    own = jnp.concatenate([dense(filter_taps), dense(signal), dense(grad_out)])
    blocks = [own]
    for step in range(1, groups):
        blocks.append(lax.ppermute(own, "seq", [(index, index ^ step) for index in range(groups)]))
    tables = [jnp.asarray(table) for table in gathered_tables(length, groups)]
    whole = pl.BlockSpec(memory_space=pltpu.VMEM)
    scalar = pl.BlockSpec(memory_space=pltpu.SMEM)
    params = pltpu.CompilerParams(vmem_limit_bytes=24 * 2**20)
    coarse = pl.pallas_call(
        functools.partial(own_kernel, channels),
        out_shape=jax.ShapeDtypeStruct((2 * rows, 3 * channels * LANES), jnp.float32),
        in_specs=[whole] * 5,
        out_specs=whole,
        compiler_params=params,
        cost_estimate=pl.CostEstimate(flops=2**27, bytes_accessed=2**21, transcendentals=0),
        name="own_part",
    )(own, *tables)
    shape = jax.ShapeDtypeStruct(dense(signal).shape, jnp.float32)
    grad_signal, grad_filter, grad_skip = pl.pallas_call(
        functools.partial(gathered_kernel, groups, channels),
        out_shape=(shape, shape, jax.ShapeDtypeStruct((channels,), jnp.float32)),
        in_specs=[scalar] + [whole] * (groups + 5),
        out_specs=(whole, whole, scalar),
        compiler_params=params,
        name="correlate",
    )(skip, coarse, *blocks, *tables)
    return (undense(grad_signal, channels), undense(grad_filter, channels), grad_skip)


def frequency_order(groups):
    slots = jnp.arange(2 * groups, dtype=jnp.int32)
    halves = slots // 2
    return jnp.where(slots % 2 == 0, halves, jnp.where(halves == 0, groups, 2 * groups - halves))


def phase_table(left_index, right_index, period):
    product = left_index[:, None] * right_index[None, :] % period
    return 2.0 * math.pi / period * product.astype(jnp.float32)


def transform_tables(cells):
    inner_len = 128
    outer_len = cells // inner_len
    outer_range = jnp.arange(outer_len, dtype=jnp.int32)
    inner_range = jnp.arange(inner_len, dtype=jnp.int32)
    outer_phase = phase_table(outer_range, outer_range, outer_len)
    twist_phase = phase_table(outer_range, inner_range, cells)
    inner_phase = phase_table(inner_range, inner_range, inner_len)
    return (
        jnp.cos(outer_phase),
        jnp.sin(outer_phase),
        jnp.cos(twist_phase),
        jnp.sin(twist_phase),
        jnp.cos(inner_phase),
        jnp.sin(inner_phase),
    )


def complex_apply(real_part, imag_part, cos_table, sin_table, pattern, turning):
    first = jnp.einsum(pattern, real_part, cos_table, precision=highest) - turning * jnp.einsum(
        pattern, imag_part, sin_table, precision=highest
    )
    second = jnp.einsum(pattern, imag_part, cos_table, precision=highest) + turning * jnp.einsum(
        pattern, real_part, sin_table, precision=highest
    )
    return (first, second)


def forward_transform(real_part, imag_part, tables):
    outer_cos, outer_sin, twist_cos, twist_sin, inner_cos, inner_sin = tables
    outer_len = outer_cos.shape[0]
    inner_len = inner_cos.shape[0]
    initial = real_part.shape
    folded = initial[:-1] + (outer_len, inner_len)
    real_part = real_part.reshape(folded)
    imag_part = imag_part.reshape(folded)
    real_part, imag_part = complex_apply(
        real_part, imag_part, outer_cos, outer_sin, "...ab,ac->...cb", -1.0
    )
    real_part, imag_part = (
        real_part * twist_cos + imag_part * twist_sin,
        imag_part * twist_cos - real_part * twist_sin,
    )
    real_part, imag_part = complex_apply(
        real_part, imag_part, inner_cos, inner_sin, "...cb,bd->...cd", -1.0
    )
    return (real_part.reshape(initial), imag_part.reshape(initial))


def inverse_transform(real_part, imag_part, tables):
    outer_cos, outer_sin, twist_cos, twist_sin, inner_cos, inner_sin = tables
    outer_len = outer_cos.shape[0]
    inner_len = inner_cos.shape[0]
    initial = real_part.shape
    folded = initial[:-1] + (outer_len, inner_len)
    real_part = real_part.reshape(folded)
    imag_part = imag_part.reshape(folded)
    real_part, imag_part = complex_apply(
        real_part, imag_part, inner_cos, inner_sin, "...cd,bd->...cb", 1.0
    )
    real_part, imag_part = (
        real_part * twist_cos - imag_part * twist_sin,
        imag_part * twist_cos + real_part * twist_sin,
    )
    real_part, imag_part = complex_apply(
        real_part, imag_part, outer_cos, outer_sin, "...cb,ac->...ab", 1.0
    )
    return (real_part.reshape(initial), imag_part.reshape(initial))


def split_body(signal, filter_taps, grad_out, skip):
    groups = lax.axis_size("seq")
    device = lax.axis_index("seq")
    cells = signal.shape[1]
    width = cells // groups
    doubled = 2 * groups
    period = doubled * cells
    freq_slots = frequency_order(groups)
    tables = transform_tables(cells)
    stacked = jnp.stack([signal, filter_taps, grad_out])[:, :, None, :]
    columns = lax.all_to_all(stacked, "seq", split_axis=3, concat_axis=2, tiled=True)
    group_rows = jnp.arange(groups, dtype=jnp.int32)
    group_phase = phase_table(group_rows, freq_slots, doubled)
    group_cos = jnp.cos(group_phase)
    group_sin = jnp.sin(group_phase)
    real_part = jnp.einsum("acpj,pm->acmj", columns, group_cos, precision=highest)
    imag_part = -jnp.einsum("acpj,pm->acmj", columns, group_sin, precision=highest)
    residues = device * width + jnp.arange(width, dtype=jnp.int32)
    twist_phase = phase_table(freq_slots, residues, period)
    twist_cos = jnp.cos(twist_phase)
    twist_sin = jnp.sin(twist_phase)
    twisted_real = real_part * twist_cos + imag_part * twist_sin
    twisted_imag = imag_part * twist_cos - real_part * twist_sin
    outgoing = jnp.stack([twisted_real, twisted_imag], 1)
    spectra = lax.all_to_all(outgoing, "seq", split_axis=3, concat_axis=4, tiled=True)
    freq_real, freq_imag = forward_transform(spectra[:, 0], spectra[:, 1], tables)
    grad_real = freq_real[-1]
    grad_imag = freq_imag[-1]
    signal_real, signal_imag = (freq_real[0], freq_imag[0])
    filter_real, filter_imag = (freq_real[1], freq_imag[1])
    input_real = filter_real * grad_real + filter_imag * grad_imag
    input_imag = filter_real * grad_imag - filter_imag * grad_real
    taps_real = signal_real * grad_real + signal_imag * grad_imag
    taps_imag = signal_real * grad_imag - signal_imag * grad_real
    back_real = jnp.stack([input_real, taps_real])
    back_imag = jnp.stack([input_imag, taps_imag])
    inverse_real, inverse_imag = inverse_transform(back_real, back_imag, tables)
    full_range = jnp.arange(cells, dtype=jnp.int32)
    local_slots = lax.dynamic_slice_in_dim(freq_slots, 2 * device, 2)
    back_phase = phase_table(local_slots, full_range, period)
    back_cos = jnp.cos(back_phase)
    back_sin = jnp.sin(back_phase)
    turned_real = inverse_real * back_cos - inverse_imag * back_sin
    turned_imag = inverse_imag * back_cos + inverse_real * back_sin
    returning = jnp.stack([turned_real, turned_imag], 1)
    residue_rows = lax.all_to_all(returning, "seq", split_axis=4, concat_axis=3, tiled=True)
    scale = 1.0 / period
    real_out = (
        jnp.einsum("ncmj,pm->ncpj", residue_rows[:, 0], group_cos, precision=highest)
        - jnp.einsum("ncmj,pm->ncpj", residue_rows[:, 1], group_sin, precision=highest)
    ) * scale
    gathered = lax.all_to_all(real_out, "seq", split_axis=2, concat_axis=3, tiled=True)
    grad_signal = gathered[0, :, 0, :] + skip[:, None] * grad_out
    grad_filter = gathered[1, :, 0, :]
    grad_skip = lax.psum(jnp.sum(grad_out * signal, axis=1), "seq")
    return (grad_signal, grad_filter, grad_skip)


def body(signal, filter_taps, grad_out, skip):
    groups = lax.axis_size("seq")
    channels, cells = signal.shape
    whole_fits = channels * cells * groups <= 2**15
    if whole_fits and groups & (groups - 1) == 0 and cells % (16 * LANES) == 0:
        return gathered_body(signal, filter_taps, grad_out, skip)
    return split_body(signal, filter_taps, grad_out, skip)
def solution(mesh):
    return jax.shard_map(
        body,
        mesh=mesh,
        in_specs=(
            P(("parts", "chan", "sub"), "seq"),
            P(("parts", "chan", "sub"), "seq"),
            P(("parts", "chan", "sub"), "seq"),
            P(("parts", "chan", "sub")),
        ),
        out_specs=(
            P(("parts", "chan", "sub"), "seq"),
            P(("parts", "chan", "sub"), "seq"),
            P(("parts", "chan", "sub")),
        ),
        check_vma=False,
    )
```

profile of v0, /device:TPU:0, one launch (start us, length us, event | category | flops | bytes accessed | tf_op | source)
XLA Modules:
  0.0 17.8 jit_solution(7437751388439485317)
XLA Ops:
  0.6 0.0 copy-start.2
  0.6 0.0 copy-start.4
  0.7 0.8 %pad_maximum_fusion.block.refs_0_ = f32[192,128]{1,0:T(8,128)S(1)} fusion(f32[64,128]{1,0:T(8,128)} %bitcast.25, f32[64,128]{1,0:T(8,128)} %bitcast.26, f32[64,128]{1,0:T(8,128)} %bitcast.27), kind=kLoop, calls=%fused_computation | loop fusion | flops 49152 | bytes 196608 | tf_op jit(solution)/shard_map/concatenate | solution.py:135
  1.5 5.1 %collective-permute-start.2 = (f32[192,128]{1,0:T(8,128)S(1)}, f32[192,128]{1,0:T(8,128)S(1)}, u32[]{:S(2)}, u32[]{:S(2)}) collective-permute-start(f32[192,128]{1,0:T(8,128)S(1)} %pad_maximum_fusion.block.refs_0_), channel_id=1, source_target_pairs={{0,12},{4,8},{8,4},{12,0},{1,13},{5,9},{9,5},{13,1},{2,14},{6,10},... | collective-permute-start | bytes 294920 | tf_op jit(solution)/shard_map/ppermute | solution.py:138
  6.6 0.0 collective-permute-start.1
  6.6 0.6 %collective-permute-start = (f32[192,128]{1,0:T(8,128)S(1)}, f32[192,128]{1,0:T(8,128)S(1)}, u32[]{:S(2)}, u32[]{:S(2)}) collective-permute-start(f32[192,128]{1,0:T(8,128)S(1)} %pad_maximum_fusion.block.refs_0_), channel_id=1, source_target_pairs={{0,4},{4,0},{8,12},{12,8},{1,5},{5,1},{9,13},{13,9},{2,6},{6,2},{1... | collective-permute-start | bytes 294920 | tf_op jit(solution)/shard_map/ppermute | solution.py:138
  7.2 0.0 copy-done.2
  7.2 0.0 copy-start
  7.2 0.9 %copy-done = bf16[2,256,256]{2,1,0:T(8,128)(2,1)S(1)} copy-done((bf16[2,256,256]{2,1,0:T(8,128)(2,1)S(1)}, bf16[2,256,256]{2,1,0:T(8,128)(2,1)}, u32[]{:S(2)}) %copy-start) | copy-done | bytes 262168
  8.2 0.0 copy-start.1
  8.2 0.9 %copy-done.1 = bf16[256,512]{1,0:T(8,128)(2,1)S(1)} copy-done((bf16[256,512]{1,0:T(8,128)(2,1)S(1)}, bf16[256,512]{1,0:T(8,128)(2,1)}, u32[]{:S(2)}) %copy-start.1) | copy-done | bytes 262168
  9.1 0.0 copy-start.3
  9.1 0.9 %copy-done.3 = f32[2,128,128]{2,1,0:T(8,128)S(1)} copy-done((f32[2,128,128]{2,1,0:T(8,128)S(1)}, f32[2,128,128]{2,1,0:T(8,128)}, u32[]{:S(2)}) %copy-start.3) | copy-done | bytes 131096
  10.0 0.2 %own_part.1.coarse_ref = f32[256,768]{1,0:T(8,128)S(1)} custom-call(f32[192,128]{1,0:T(8,128)S(1)} %pad_maximum_fusion.block.refs_0_, bf16[256,512]{1,0:T(8,128)(2,1)S(1)} %copy-done.1, f32[2,128,128]{2,1,0:T(8,128)S(1)} %copy-done.3, bf16[2,256,256]{2,1,0:T(8,128)(2,1)S(1)} %copy-done, bf16[4,2,32,256]{3,2,1,0:T(8,128)(2,1)S(1)} %copy-done.2), custom_call_target="tpu_custom_call" | custom-call | flops 134217728 | bytes 2097152 | tf_op jit(solution)/shard_map/own_part/pallas_call | solution.py:143
  10.3 0.0 collective-permute-done.2.refs_3_
  10.3 4.6 %collective-permute-done.1.refs_2_ = f32[192,128]{1,0:T(8,128)S(1)} collective-permute-done((f32[192,128]{1,0:T(8,128)S(1)}, f32[192,128]{1,0:T(8,128)S(1)}, u32[]{:S(2)}, u32[]{:S(2)}) %collective-permute-start.1) | collective-permute-done | bytes 98336 | tf_op jit(solution)/shard_map/ppermute | solution.py:138
  14.8 0.0 collective-permute-done.refs_1_
  14.8 0.0 copy-done.4
  14.9 2.9 %correlate.1 = (f32[64,128]{1,0:T(8,128)}, f32[64,128]{1,0:T(8,128)}, f32[2]{0:T(128)}) custom-call(f32[2]{0:T(128)S(1)} %copy-done.4, f32[256,768]{1,0:T(8,128)S(1)} %own_part.1.coarse_ref, f32[192,128]{1,0:T(8,128)S(1)} %pad_maximum_fusion.block.refs_0_, f32[192,128]{1,0:T(8,128)S(1)} %collective-permute-done.refs_1_, ...), custom_call_target="tpu_custom_call" | custom-call | tf_op jit(solution)/shard_map/correlate/pallas_call | solution.py:153
Async XLA Ops:
  0.6 6.6 %copy-start.2 = (bf16[4,2,32,256]{3,2,1,0:T(8,128)(2,1)S(1)}, bf16[4,2,32,256]{3,2,1,0:T(8,128)(2,1)}, u32[]{:S(2)}) copy-start(bf16[4,2,32,256]{3,2,1,0:T(8,128)(2,1)} %constant.11.clone.last.refs_7_) | copy-start | bytes 393220
  0.6 14.2 %copy-start.4 = (f32[2]{0:T(128)S(1)}, f32[2]{0:T(128)}, u32[]{:S(2)}) copy-start(f32[2]{0:T(128)} %skip_ref.1) | copy-start | bytes 28
  1.5 8.8 %collective-permute-start.2 = (f32[192,128]{1,0:T(8,128)S(1)}, f32[192,128]{1,0:T(8,128)S(1)}, u32[]{:S(2)}, u32[]{:S(2)}) collective-permute-start(f32[192,128]{1,0:T(8,128)S(1)} %pad_maximum_fusion.block.refs_0_), channel_id=1, source_target_pairs={{0,12},{4,8},{8,4},{12,0},{1,13},{5,9},{9,5},{13,1},{2,14},{6,10},... | collective-permute-start | bytes 294920 | tf_op jit(solution)/shard_map/ppermute | solution.py:138
  6.6 8.3 %collective-permute-start.1 = (f32[192,128]{1,0:T(8,128)S(1)}, f32[192,128]{1,0:T(8,128)S(1)}, u32[]{:S(2)}, u32[]{:S(2)}) collective-permute-start(f32[192,128]{1,0:T(8,128)S(1)} %pad_maximum_fusion.block.refs_0_), channel_id=1, source_target_pairs={{0,8},{4,12},{8,0},{12,4},{1,9},{5,13},{9,1},{13,5},{2,10},{6,14},... | collective-permute-start | bytes 294920 | tf_op jit(solution)/shard_map/ppermute | solution.py:138
  6.6 8.3 %collective-permute-start = (f32[192,128]{1,0:T(8,128)S(1)}, f32[192,128]{1,0:T(8,128)S(1)}, u32[]{:S(2)}, u32[]{:S(2)}) collective-permute-start(f32[192,128]{1,0:T(8,128)S(1)} %pad_maximum_fusion.block.refs_0_), channel_id=1, source_target_pairs={{0,4},{4,0},{8,12},{12,8},{1,5},{5,1},{9,13},{13,9},{2,6},{6,2},{1... | collective-permute-start | bytes 294920 | tf_op jit(solution)/shard_map/ppermute | solution.py:138
  7.2 1.0 %copy-start = (bf16[2,256,256]{2,1,0:T(8,128)(2,1)S(1)}, bf16[2,256,256]{2,1,0:T(8,128)(2,1)}, u32[]{:S(2)}) copy-start(bf16[2,256,256]{2,1,0:T(8,128)(2,1)} %constant.10.clone.second.refs_6_) | copy-start | bytes 786436
  8.2 0.9 %copy-start.1 = (bf16[256,512]{1,0:T(8,128)(2,1)S(1)}, bf16[256,512]{1,0:T(8,128)(2,1)}, u32[]{:S(2)}) copy-start(bf16[256,512]{1,0:T(8,128)(2,1)} %constant.8.clone.first.refs_4_) | copy-start | bytes 786436
  9.1 0.9 %copy-start.3 = (f32[2,128,128]{2,1,0:T(8,128)S(1)}, f32[2,128,128]{2,1,0:T(8,128)}, u32[]{:S(2)}) copy-start(f32[2,128,128]{2,1,0:T(8,128)} %constant.9.clone.twiddle.refs_5_) | copy-start | bytes 393220
where the time goes:
time: 18 us; the launch traced here: 17.8 us
  starting transfers between devices  5.73 us (32%)
  waiting for transfers between devices  4.56 us (25%)
  Pallas kernels  3.14 us (17%)
  local copies, waits for them, and re-layouts  2.81 us (16%)
  other arithmetic  0.83 us (5%)
  between operations  0.67 us (4%)
    ppermute x3, starting transfers between devices, gathered_body(): lax.ppermute(own, 'seq', [(index, index ^ step) for index in range(groups)])  5.73 us
    ppermute x3, waiting for transfers between devices, gathered_body(): lax.ppermute(own, 'seq', [(index, index ^ step) for index in range(groups)])  4.56 us
    pallas_call x1, Pallas kernels, gathered_body(): pl.pallas_call(functools.partial(gathered_kernel, groups, channels), out_...  2.91 us
    unnamed x10, local copies, waits for them, and re-layouts  2.81 us
    concatenate x1, other arithmetic, gathered_body(): own = jnp.concatenate([dense(filter_taps), dense(signal), dense(grad_out)])  0.83 us
  transfers between devices with their start and end apart: 3, of which 1 were waited for; matrix products, arithmetic and copies ran while one was open for 0% of the time, Pallas kernels for 1%

commit v1 on v0

--- a/solution.py
+++ b/solution.py
@@ -47,7 +47,7 @@
 
 
 def product(left, right):
-    return dot(left[0], right[0]) + dot(left[0], right[1]) + dot(left[1], right[0])
+    return dot(jnp.concatenate([left[0], left[0], left[1]], axis=1), jnp.concatenate([right[0], right[1], right[0]]))
 
 
 def stage_rows(block, channels):
@@ -66,6 +66,20 @@
     return table[:, pl.ds(pl.multiple_of(group * width, width), width)]
 
 
+def cycle_entry(index):
+    return index ^ (index >> 1)
+
+
+def sender(device, step, groups):
+    place = device
+    shift = 1
+    while 1 << shift < groups:
+        place = lax.bitwise_xor(place, lax.shift_right_logical(device, shift))
+        shift += 1
+    place = lax.rem(place + (groups - step), groups)
+    return lax.bitwise_xor(place, lax.shift_right_logical(place, 1))
+
+
 def own_kernel(channels, block, first, twiddle, second, last, out_ref):
     out_ref[...] = dot(stage_columns(first, lax.axis_index("seq")), stage_rows(block, channels))
 
@@ -74,37 +88,57 @@
     blocks = refs[:groups]
     first, twiddle, second, last = refs[groups : groups + 4]
     grad_signal_ref, grad_filter_ref, grad_skip_ref = refs[groups + 4 :]
+    skips = skip_ref[...]
     device = lax.axis_index("seq")
     rows = twiddle.shape[1]
     height = rows // groups
 
-    columns = [stage_columns(first, lax.bitwise_xor(device, step)) for step in range(1, groups)]
-    data = [stage_rows(block, channels) for block in blocks[1:]]
-    coarse = coarse_ref[...] + dot(jnp.concatenate(columns, axis=1), jnp.concatenate(data))
+    senders = [sender(device, step, groups) for step in reversed(range(1, groups))]
+    columns = jnp.concatenate([stage_columns(first, index) for index in senders], axis=1)
     cos, sin = twiddle[0], twiddle[1]
-    turned = []
-    for index in range(3 * channels):
-        lanes = slice(index * LANES, (index + 1) * LANES)
-        real, imag = coarse[:rows, lanes], coarse[rows:, lanes]
-        turned.append(jnp.concatenate([real * cos + imag * sin, imag * cos - real * sin], axis=1))
-    spectra = product(split(jnp.concatenate(turned)), (second[0], second[1]))
-    products = []
-    for channel in range(channels):
-        grad = spectra[(3 * channel + 2) * rows : (3 * channel + 3) * rows]
+    data = jnp.concatenate([stage_rows(block, channels) for block in blocks[1:]])
+
+    def stage1(channel):
+        lanes = slice(3 * channel * LANES, 3 * (channel + 1) * LANES)
+        return coarse_ref[:, lanes] + dot(columns, data[:, lanes])
+
+    def turn_out(coarse):
+        part = []
+        for array in range(3):
+            lanes = slice(array * LANES, (array + 1) * LANES)
+            real, imag = coarse[:rows, lanes], coarse[rows:, lanes]
+            part.append(jnp.concatenate([real * cos + imag * sin, imag * cos - real * sin], axis=1))
+        return split(jnp.concatenate(part))
+
+    def wide(value):
+        return product(value, (second[0], second[1]))
+
+    def mix(spectra):
+        grad = spectra[2 * rows :]
         grad_real, grad_imag = grad[:, :LANES], grad[:, LANES:]
+        part = []
         for array in range(2):
-            other = spectra[(3 * channel + array) * rows : (3 * channel + array + 1) * rows]
+            other = spectra[array * rows : (array + 1) * rows]
             real, imag = other[:, :LANES], other[:, LANES:]
-            products.append(
+            part.append(
                 jnp.concatenate([real * grad_real + imag * grad_imag, imag * grad_real - real * grad_imag], axis=1)
             )
-    back = product(split(jnp.concatenate(products)), (second[0], second[1]))
-    spread = []
-    for index in range(2 * channels):
-        value = back[index * rows : (index + 1) * rows]
-        real, minus = value[:, :LANES], value[:, LANES:]
-        spread.append(jnp.concatenate([real * cos + minus * sin, real * sin - minus * cos]))
-    result = product((last[device, 0], last[device, 1]), split(jnp.concatenate(spread, axis=1)))
+        return split(jnp.concatenate(part))
+
+    def turn_back(back):
+        spread = []
+        for array in range(2):
+            value = back[array * rows : (array + 1) * rows]
+            real, minus = value[:, :LANES], value[:, LANES:]
+            spread.append(jnp.concatenate([real * cos + minus * sin, real * sin - minus * cos]))
+        return split(jnp.concatenate(spread, axis=1))
+
+    turned = [turn_out(stage1(channel)) for channel in range(channels)]
+    spectra = [wide(value) for value in turned]
+    mixed = [mix(value) for value in spectra]
+    back = [wide(value) for value in mixed]
+    spread = [turn_back(value) for value in back]
+    result = jnp.concatenate([product((last[device, 0], last[device, 1]), value) for value in spread], axis=1)
 
     cells = height * channels
     total = sum(block[cells : 2 * cells] * block[2 * cells :] for block in blocks)
@@ -113,7 +147,7 @@
         grad_skip_ref[channel] = jnp.sum(jnp.where(owner == channel, total, 0.0))
         mine = pl.ds(channel, height, stride=channels)
         lanes = 2 * channel * LANES
-        kept = skip_ref[channel] * blocks[0][pl.ds(2 * cells + channel, height, stride=channels)]
+        kept = skips[channel] * blocks[0][pl.ds(2 * cells + channel, height, stride=channels)]
         grad_signal_ref[mine, :] = result[:, lanes : lanes + LANES] + kept
         grad_filter_ref[mine, :] = result[:, lanes + LANES : lanes + 2 * LANES]
 
@@ -134,8 +168,9 @@
     rows = length // LANES
     own = jnp.concatenate([dense(filter_taps), dense(signal), dense(grad_out)])
     blocks = [own]
-    for step in range(1, groups):
-        blocks.append(lax.ppermute(own, "seq", [(index, index ^ step) for index in range(groups)]))
+    for step in reversed(range(1, groups)):
+        hops = [(cycle_entry(index), cycle_entry((index + step) % groups)) for index in range(groups)]
+        blocks.append(lax.ppermute(own, "seq", hops))
     tables = [jnp.asarray(table) for table in gathered_tables(length, groups)]
     whole = pl.BlockSpec(memory_space=pltpu.VMEM)
     scalar = pl.BlockSpec(memory_space=pltpu.SMEM)
@@ -153,7 +188,7 @@
     grad_signal, grad_filter, grad_skip = pl.pallas_call(
         functools.partial(gathered_kernel, groups, channels),
         out_shape=(shape, shape, jax.ShapeDtypeStruct((channels,), jnp.float32)),
-        in_specs=[scalar] + [whole] * (groups + 5),
+        in_specs=[whole] + [whole] * (groups + 5),
         out_specs=(whole, whole, scalar),
         compiler_params=params,
         name="correlate",

time: 18 us -> 15.6 us (0.87)
  the two profiles are of different devices: /device:TPU:0 before, /device:TPU:22 now
where the time goes in v1:
time: 15.6 us; the launch traced here: 15.4 us
  waiting for transfers between devices  5.43 us (35%)
  starting transfers between devices  3.41 us (22%)
  local copies, waits for them, and re-layouts  2.81 us (18%)
  Pallas kernels  2.21 us (14%)
  other arithmetic  0.83 us (5%)
  between operations  0.67 us (4%)
    ppermute x3, waiting for transfers between devices, gathered_body(): blocks.append(lax.ppermute(own, 'seq', hops))  5.43 us
    ppermute x3, starting transfers between devices, gathered_body(): blocks.append(lax.ppermute(own, 'seq', hops))  3.41 us
    unnamed x10, local copies, waits for them, and re-layouts  2.81 us
    pallas_call x1, Pallas kernels, gathered_body(): pl.pallas_call(functools.partial(gathered_kernel, groups, channels), out_...  1.97 us
    concatenate x1, other arithmetic, gathered_body(): own = jnp.concatenate([dense(filter_taps), dense(signal), dense(grad_out)])  0.83 us
  transfers between devices with their start and end apart: 3, of which 1 were waited for; matrix products, arithmetic and copies ran while one was open for 0% of the time, Pallas kernels for 2%

profile of v1, /device:TPU:22, one launch (start us, length us, event | category | flops | bytes accessed | tf_op | source)
XLA Modules:
  0.0 15.4 jit_solution(16216978839904513577)
XLA Ops:
  0.6 0.0 copy-start.2
  0.6 0.0 copy-start.4
  0.7 0.8 %pad_maximum_fusion.block.refs_0_ = f32[192,128]{1,0:T(8,128)S(1)} fusion(f32[64,128]{1,0:T(8,128)} %bitcast.25, f32[64,128]{1,0:T(8,128)} %bitcast.26, f32[64,128]{1,0:T(8,128)} %bitcast.27), kind=kLoop, calls=%fused_computation | loop fusion | flops 49152 | bytes 196608 | tf_op jit(solution)/shard_map/concatenate | solution.py:169
  1.5 0.4 %collective-permute-start.2 = (f32[192,128]{1,0:T(8,128)S(1)}, f32[192,128]{1,0:T(8,128)S(1)}, u32[]{:S(2)}, u32[]{:S(2)}) collective-permute-start(f32[192,128]{1,0:T(8,128)S(1)} %pad_maximum_fusion.block.refs_0_), channel_id=1, source_target_pairs={{0,4},{4,12},{12,8},{8,0},{1,5},{5,13},{13,9},{9,1},{2,6},{6,14},{... | collective-permute-start | bytes 294920 | tf_op jit(solution)/shard_map/ppermute | solution.py:173
  1.9 2.7 %collective-permute-start.1 = (f32[192,128]{1,0:T(8,128)S(1)}, f32[192,128]{1,0:T(8,128)S(1)}, u32[]{:S(2)}, u32[]{:S(2)}) collective-permute-start(f32[192,128]{1,0:T(8,128)S(1)} %pad_maximum_fusion.block.refs_0_), channel_id=1, source_target_pairs={{0,12},{4,8},{12,0},{8,4},{1,13},{5,9},{13,1},{9,5},{2,14},{6,10},... | collective-permute-start | bytes 294920 | tf_op jit(solution)/shard_map/ppermute | solution.py:173
  4.6 0.3 %collective-permute-start = (f32[192,128]{1,0:T(8,128)S(1)}, f32[192,128]{1,0:T(8,128)S(1)}, u32[]{:S(2)}, u32[]{:S(2)}) collective-permute-start(f32[192,128]{1,0:T(8,128)S(1)} %pad_maximum_fusion.block.refs_0_), channel_id=1, source_target_pairs={{0,8},{4,0},{12,4},{8,12},{1,9},{5,1},{13,5},{9,13},{2,10},{6,2},{... | collective-permute-start | bytes 294920 | tf_op jit(solution)/shard_map/ppermute | solution.py:173
  4.9 0.0 copy-done.2
  4.9 0.0 copy-start
  4.9 0.9 %copy-done = bf16[2,256,256]{2,1,0:T(8,128)(2,1)S(1)} copy-done((bf16[2,256,256]{2,1,0:T(8,128)(2,1)S(1)}, bf16[2,256,256]{2,1,0:T(8,128)(2,1)}, u32[]{:S(2)}) %copy-start) | copy-done | bytes 262168
  5.8 0.0 copy-start.1
  5.8 0.9 %copy-done.1 = bf16[256,512]{1,0:T(8,128)(2,1)S(1)} copy-done((bf16[256,512]{1,0:T(8,128)(2,1)S(1)}, bf16[256,512]{1,0:T(8,128)(2,1)}, u32[]{:S(2)}) %copy-start.1) | copy-done | bytes 262168
  6.8 0.0 copy-start.3
  6.8 0.9 %copy-done.3 = f32[2,128,128]{2,1,0:T(8,128)S(1)} copy-done((f32[2,128,128]{2,1,0:T(8,128)S(1)}, f32[2,128,128]{2,1,0:T(8,128)}, u32[]{:S(2)}) %copy-start.3) | copy-done | bytes 131096
  7.7 0.2 %own_part.1.coarse_ref = f32[256,768]{1,0:T(8,128)S(1)} custom-call(f32[192,128]{1,0:T(8,128)S(1)} %pad_maximum_fusion.block.refs_0_, bf16[256,512]{1,0:T(8,128)(2,1)S(1)} %copy-done.1, f32[2,128,128]{2,1,0:T(8,128)S(1)} %copy-done.3, bf16[2,256,256]{2,1,0:T(8,128)(2,1)S(1)} %copy-done, bf16[4,2,32,256]{3,2,1,0:T(8,128)(2,1)S(1)} %copy-done.2), custom_call_target="tpu_custom_call" | custom-call | flops 134217728 | bytes 2097152 | tf_op jit(solution)/shard_map/own_part/pallas_call | solution.py:178
  8.0 0.0 collective-permute-done.2.refs_3_
  8.0 5.4 %collective-permute-done.1.refs_2_ = f32[192,128]{1,0:T(8,128)S(1)} collective-permute-done((f32[192,128]{1,0:T(8,128)S(1)}, f32[192,128]{1,0:T(8,128)S(1)}, u32[]{:S(2)}, u32[]{:S(2)}) %collective-permute-start.1) | collective-permute-done | bytes 98336 | tf_op jit(solution)/shard_map/ppermute | solution.py:173
  13.4 0.0 collective-permute-done.refs_1_
  13.4 0.0 copy-done.4
  13.4 2.0 %correlate.1 = (f32[64,128]{1,0:T(8,128)}, f32[64,128]{1,0:T(8,128)}, f32[2]{0:T(128)}) custom-call(f32[2]{0:T(128)S(1)} %copy-done.4, f32[256,768]{1,0:T(8,128)S(1)} %own_part.1.coarse_ref, f32[192,128]{1,0:T(8,128)S(1)} %pad_maximum_fusion.block.refs_0_, f32[192,128]{1,0:T(8,128)S(1)} %collective-permute-done.refs_1_, ...), custom_call_target="tpu_custom_call" | custom-call | tf_op jit(solution)/shard_map/correlate/pallas_call | solution.py:188
Async XLA Ops:
  0.6 4.3 %copy-start.2 = (bf16[4,2,32,256]{3,2,1,0:T(8,128)(2,1)S(1)}, bf16[4,2,32,256]{3,2,1,0:T(8,128)(2,1)}, u32[]{:S(2)}) copy-start(bf16[4,2,32,256]{3,2,1,0:T(8,128)(2,1)} %constant.11.clone.last.refs_7_) | copy-start | bytes 393220
  0.6 12.7 %copy-start.4 = (f32[2]{0:T(128)S(1)}, f32[2]{0:T(128)}, u32[]{:S(2)}) copy-start(f32[2]{0:T(128)} %skip_ref.1) | copy-start | bytes 28
  1.5 6.5 %collective-permute-start.2 = (f32[192,128]{1,0:T(8,128)S(1)}, f32[192,128]{1,0:T(8,128)S(1)}, u32[]{:S(2)}, u32[]{:S(2)}) collective-permute-start(f32[192,128]{1,0:T(8,128)S(1)} %pad_maximum_fusion.block.refs_0_), channel_id=1, source_target_pairs={{0,4},{4,12},{12,8},{8,0},{1,5},{5,13},{13,9},{9,1},{2,6},{6,14},{... | collective-permute-start | bytes 294920 | tf_op jit(solution)/shard_map/ppermute | solution.py:173
  1.9 11.5 %collective-permute-start.1 = (f32[192,128]{1,0:T(8,128)S(1)}, f32[192,128]{1,0:T(8,128)S(1)}, u32[]{:S(2)}, u32[]{:S(2)}) collective-permute-start(f32[192,128]{1,0:T(8,128)S(1)} %pad_maximum_fusion.block.refs_0_), channel_id=1, source_target_pairs={{0,12},{4,8},{12,0},{8,4},{1,13},{5,9},{13,1},{9,5},{2,14},{6,10},... | collective-permute-start | bytes 294920 | tf_op jit(solution)/shard_map/ppermute | solution.py:173
  4.6 8.8 %collective-permute-start = (f32[192,128]{1,0:T(8,128)S(1)}, f32[192,128]{1,0:T(8,128)S(1)}, u32[]{:S(2)}, u32[]{:S(2)}) collective-permute-start(f32[192,128]{1,0:T(8,128)S(1)} %pad_maximum_fusion.block.refs_0_), channel_id=1, source_target_pairs={{0,8},{4,0},{12,4},{8,12},{1,9},{5,1},{13,5},{9,13},{2,10},{6,2},{... | collective-permute-start | bytes 294920 | tf_op jit(solution)/shard_map/ppermute | solution.py:173
  4.9 1.0 %copy-start = (bf16[2,256,256]{2,1,0:T(8,128)(2,1)S(1)}, bf16[2,256,256]{2,1,0:T(8,128)(2,1)}, u32[]{:S(2)}) copy-start(bf16[2,256,256]{2,1,0:T(8,128)(2,1)} %constant.10.clone.second.refs_6_) | copy-start | bytes 786436
  5.8 0.9 %copy-start.1 = (bf16[256,512]{1,0:T(8,128)(2,1)S(1)}, bf16[256,512]{1,0:T(8,128)(2,1)}, u32[]{:S(2)}) copy-start(bf16[256,512]{1,0:T(8,128)(2,1)} %constant.8.clone.first.refs_4_) | copy-start | bytes 786436
  6.8 0.9 %copy-start.3 = (f32[2,128,128]{2,1,0:T(8,128)S(1)}, f32[2,128,128]{2,1,0:T(8,128)}, u32[]{:S(2)}) copy-start(f32[2,128,128]{2,1,0:T(8,128)} %constant.9.clone.twiddle.refs_5_) | copy-start | bytes 393220

commit v2 on v1

--- a/solution.py
+++ b/solution.py
@@ -34,7 +34,7 @@
     angle = 2.0 * np.pi / LANES * fine[:, None] * fine[None, :]
     cos, sin = np.cos(angle), np.sin(angle)
     second = np.block([[cos, -sin], [sin, cos]])
-    return stage_first, twiddle, np.stack(split_table(second)), np.stack(split_table(last), axis=1)
+    return stage_first, twiddle, np.stack(split_table(second)), np.concatenate(split_table(last), axis=1)
 
 
 def split(value):
@@ -66,25 +66,38 @@
     return table[:, pl.ds(pl.multiple_of(group * width, width), width)]
 
 
-def cycle_entry(index):
-    return index ^ (index >> 1)
-
-
-def sender(device, step, groups):
-    place = device
-    shift = 1
-    while 1 << shift < groups:
-        place = lax.bitwise_xor(place, lax.shift_right_logical(device, shift))
-        shift += 1
-    place = lax.rem(place + (groups - step), groups)
-    return lax.bitwise_xor(place, lax.shift_right_logical(place, 1))
+def routes(groups, cores):
+    plans = [(tuple(range(groups)), tuple(range(1, groups)))]
+    if groups == 4:
+        plans = [((0, 2, 1, 3), (3, 1, 2)), ((0, 1, 3, 2), (1, 2, 3))]
+    steps = []
+    for index in range(groups - 1):
+        targets = []
+        for core in range(cores):
+            cycle, moves = plans[core % len(plans)]
+            ahead = {cycle[place]: cycle[(place + moves[index]) % groups] for place in range(groups)}
+            targets.append([ahead[device] for device in range(groups)])
+        steps.append(targets)
+    return steps
+
+
+def sender(targets):
+    code = 0
+    for core, ahead in enumerate(targets):
+        packed = sum(device << 4 * target for device, target in enumerate(ahead))
+        code = jnp.where(lax.axis_index("sub") == core, packed, code)
+    return lax.bitwise_and(lax.shift_right_logical(code, 4 * lax.axis_index("seq")), 15)
 
 
 def own_kernel(channels, block, first, twiddle, second, last, out_ref):
     out_ref[...] = dot(stage_columns(first, lax.axis_index("seq")), stage_rows(block, channels))
 
 
-def gathered_kernel(groups, channels, skip_ref, coarse_ref, *refs):
+def early_kernel(channels, targets, coarse_ref, block, first, out_ref):
+    out_ref[...] = coarse_ref[...] + dot(stage_columns(first, sender(targets)), stage_rows(block, channels))
+
+
+def gathered_kernel(groups, channels, late, skip_ref, coarse_ref, *refs):
     blocks = refs[:groups]
     first, twiddle, second, last = refs[groups : groups + 4]
     grad_signal_ref, grad_filter_ref, grad_skip_ref = refs[groups + 4 :]
@@ -93,10 +106,10 @@
     rows = twiddle.shape[1]
     height = rows // groups
 
-    senders = [sender(device, step, groups) for step in reversed(range(1, groups))]
-    columns = jnp.concatenate([stage_columns(first, index) for index in senders], axis=1)
+    columns = jnp.concatenate([stage_columns(first, sender(targets)) for targets in late], axis=1)
+    data = jnp.concatenate([stage_rows(block, channels) for block in blocks[groups - len(late) :]])
     cos, sin = twiddle[0], twiddle[1]
-    data = jnp.concatenate([stage_rows(block, channels) for block in blocks[1:]])
+    last_rows = last[device]
 
     def stage1(channel):
         lanes = slice(3 * channel * LANES, 3 * (channel + 1) * LANES)
@@ -133,12 +146,16 @@
             spread.append(jnp.concatenate([real * cos + minus * sin, real * sin - minus * cos]))
         return split(jnp.concatenate(spread, axis=1))
 
+    def narrow(value):
+        both = dot(last_rows, value[0])
+        return both[:height] + both[height:] + dot(last_rows[:height], value[1])
+
     turned = [turn_out(stage1(channel)) for channel in range(channels)]
     spectra = [wide(value) for value in turned]
     mixed = [mix(value) for value in spectra]
     back = [wide(value) for value in mixed]
     spread = [turn_back(value) for value in back]
-    result = jnp.concatenate([product((last[device, 0], last[device, 1]), value) for value in spread], axis=1)
+    result = jnp.concatenate([narrow(value) for value in spread], axis=1)
 
     cells = height * channels
     total = sum(block[cells : 2 * cells] * block[2 * cells :] for block in blocks)
@@ -167,10 +184,14 @@
     length = cells * groups
     rows = length // LANES
     own = jnp.concatenate([dense(filter_taps), dense(signal), dense(grad_out)])
-    blocks = [own]
-    for step in reversed(range(1, groups)):
-        hops = [(cycle_entry(index), cycle_entry((index + step) % groups)) for index in range(groups)]
-        blocks.append(lax.ppermute(own, "seq", hops))
+    cores = lax.axis_size("sub")
+    steps = routes(groups, cores)
+    arrived = []
+    for targets in reversed(steps):
+        hops = []
+        for core, ahead in enumerate(targets):
+            hops += [(device * cores + core, target * cores + core) for device, target in enumerate(ahead)]
+        arrived.insert(0, lax.ppermute(own, ("seq", "sub"), hops))
     tables = [jnp.asarray(table) for table in gathered_tables(length, groups)]
     whole = pl.BlockSpec(memory_space=pltpu.VMEM)
     scalar = pl.BlockSpec(memory_space=pltpu.SMEM)
@@ -184,15 +205,24 @@
         cost_estimate=pl.CostEstimate(flops=2**27, bytes_accessed=2**21, transcendentals=0),
         name="own_part",
     )(own, *tables)
+    coarse = pl.pallas_call(
+        functools.partial(early_kernel, channels, steps[0]),
+        out_shape=jax.ShapeDtypeStruct(coarse.shape, jnp.float32),
+        in_specs=[whole] * 3,
+        out_specs=whole,
+        compiler_params=params,
+        cost_estimate=pl.CostEstimate(flops=2**27, bytes_accessed=2**21, transcendentals=0),
+        name="early_part",
+    )(coarse, arrived[0], tables[0])
     shape = jax.ShapeDtypeStruct(dense(signal).shape, jnp.float32)
     grad_signal, grad_filter, grad_skip = pl.pallas_call(
-        functools.partial(gathered_kernel, groups, channels),
+        functools.partial(gathered_kernel, groups, channels, steps[1:]),
         out_shape=(shape, shape, jax.ShapeDtypeStruct((channels,), jnp.float32)),
         in_specs=[whole] + [whole] * (groups + 5),
         out_specs=(whole, whole, scalar),
         compiler_params=params,
         name="correlate",
-    )(skip, coarse, *blocks, *tables)
+    )(skip, coarse, own, *arrived, *tables)
     return (undense(grad_signal, channels), undense(grad_filter, channels), grad_skip)
 
 
@@ -339,7 +369,7 @@
     groups = lax.axis_size("seq")
     channels, cells = signal.shape
     whole_fits = channels * cells * groups <= 2**15
-    if whole_fits and groups & (groups - 1) == 0 and cells % (16 * LANES) == 0:
+    if whole_fits and groups <= 8 and cells % (16 * LANES) == 0:
         return gathered_body(signal, filter_taps, grad_out, skip)
     return split_body(signal, filter_taps, grad_out, skip)
 def solution(mesh):

time: 15.6 us -> 15.3 us (0.981)
  the two profiles are of different devices: /device:TPU:22 before, /device:TPU:24 now
where the time goes in v2:
time: 15.3 us; the launch traced here: 15.1 us
  waiting for transfers between devices  4.61 us (30%)
  starting transfers between devices  3.86 us (25%)
  local copies, waits for them, and re-layouts  2.82 us (18%)
  Pallas kernels  2.34 us (15%)
  other arithmetic  0.83 us (5%)
  between operations  0.67 us (4%)
    ppermute x3, waiting for transfers between devices, gathered_body(): arrived.insert(0, lax.ppermute(own, ('seq', 'sub'), hops))  4.61 us
    ppermute x3, starting transfers between devices, gathered_body(): arrived.insert(0, lax.ppermute(own, ('seq', 'sub'), hops))  3.86 us
    unnamed x10, local copies, waits for them, and re-layouts  2.82 us
    pallas_call x1, Pallas kernels, gathered_body(): pl.pallas_call(functools.partial(gathered_kernel, groups, channels, steps...  1.85 us
    concatenate x1, other arithmetic, gathered_body(): own = jnp.concatenate([dense(filter_taps), dense(signal), dense(grad_out)])  0.83 us
  transfers between devices with their start and end apart: 3, of which 2 were waited for; matrix products, arithmetic and copies ran while one was open for 0% of the time, Pallas kernels for 3%

profile of v2, /device:TPU:24, one launch (start us, length us, event | category | flops | bytes accessed | tf_op | source)
XLA Modules:
  0.0 15.1 jit_solution(7766496879943779112)
XLA Ops:
  0.6 0.0 copy-start.2
  0.6 0.8 %pad_maximum_fusion.block.refs_0_ = f32[192,128]{1,0:T(8,128)S(1)} fusion(f32[64,128]{1,0:T(8,128)} %bitcast.25, f32[64,128]{1,0:T(8,128)} %bitcast.26, f32[64,128]{1,0:T(8,128)} %bitcast.27), kind=kLoop, calls=%fused_computation | loop fusion | flops 49152 | bytes 196608 | tf_op jit(solution)/shard_map/concatenate | solution.py:186
  1.5 0.4 %collective-permute-start = (f32[192,128]{1,0:T(8,128)S(1)}, f32[192,128]{1,0:T(8,128)S(1)}, u32[]{:S(2)}, u32[]{:S(2)}) collective-permute-start(f32[192,128]{1,0:T(8,128)S(1)} %pad_maximum_fusion.block.refs_0_), channel_id=1, source_target_pairs={{0,12},{4,8},{8,0},{12,4},{1,5},{5,13},{9,1},{13,9},{2,14},{6,10},... | collective-permute-start | bytes 294920 | tf_op jit(solution)/shard_map/ppermute | solution.py:194
  1.8 3.5 %collective-permute-start.1 = (f32[192,128]{1,0:T(8,128)S(1)}, f32[192,128]{1,0:T(8,128)S(1)}, u32[]{:S(2)}, u32[]{:S(2)}) collective-permute-start(f32[192,128]{1,0:T(8,128)S(1)} %pad_maximum_fusion.block.refs_0_), channel_id=1, source_target_pairs={{0,8},{4,12},{8,4},{12,0},{1,13},{5,9},{9,5},{13,1},{2,10},{6,14},... | collective-permute-start | bytes 294920 | tf_op jit(solution)/shard_map/ppermute | solution.py:194
  5.3 0.0 collective-permute-start.2
  5.3 0.0 copy-done.2
  5.3 0.0 copy-start
  5.3 0.9 %copy-done = bf16[256,512]{1,0:T(8,128)(2,1)S(1)} copy-done((bf16[256,512]{1,0:T(8,128)(2,1)S(1)}, bf16[256,512]{1,0:T(8,128)(2,1)}, u32[]{:S(2)}) %copy-start) | copy-done | bytes 262168
  6.3 0.0 copy-start.1
  6.3 0.9 %copy-done.1 = bf16[2,256,256]{2,1,0:T(8,128)(2,1)S(1)} copy-done((bf16[2,256,256]{2,1,0:T(8,128)(2,1)S(1)}, bf16[2,256,256]{2,1,0:T(8,128)(2,1)}, u32[]{:S(2)}) %copy-start.1) | copy-done | bytes 262168
  7.2 0.0 copy-start.3
  7.2 0.9 %copy-done.3 = f32[2,128,128]{2,1,0:T(8,128)S(1)} copy-done((f32[2,128,128]{2,1,0:T(8,128)S(1)}, f32[2,128,128]{2,1,0:T(8,128)}, u32[]{:S(2)}) %copy-start.3) | copy-done | bytes 131096
  8.1 0.2 %own_part.1.coarse_ref = f32[256,768]{1,0:T(8,128)S(1)} custom-call(f32[192,128]{1,0:T(8,128)S(1)} %pad_maximum_fusion.block.refs_0_, bf16[256,512]{1,0:T(8,128)(2,1)S(1)} %copy-done, f32[2,128,128]{2,1,0:T(8,128)S(1)} %copy-done.3, bf16[2,256,256]{2,1,0:T(8,128)(2,1)S(1)} %copy-done.1, bf16[4,64,256]{2,1,0:T(8,128)(2,1)S(1)} %copy-done.2), custom_call_target="tpu_custom_call" | custom-call | flops 134217728 | bytes 2097152 | tf_op jit(solution)/shard_map/own_part/pallas_call | solution.py:199
  8.4 0.0 copy-start.4
  8.4 0.6 %collective-permute-done.block.refs_1_ = f32[192,128]{1,0:T(8,128)S(1)} collective-permute-done((f32[192,128]{1,0:T(8,128)S(1)}, f32[192,128]{1,0:T(8,128)S(1)}, u32[]{:S(2)}, u32[]{:S(2)}) %collective-permute-start) | collective-permute-done | bytes 98336 | tf_op jit(solution)/shard_map/ppermute | solution.py:194
  9.0 0.2 %early_part.1.coarse_ref = f32[256,768]{1,0:T(8,128)S(1)} custom-call(f32[256,768]{1,0:T(8,128)S(1)} %own_part.1.coarse_ref, f32[192,128]{1,0:T(8,128)S(1)} %collective-permute-done.block.refs_1_, bf16[256,512]{1,0:T(8,128)(2,1)S(1)} %copy-done), custom_call_target="tpu_custom_call" | custom-call | flops 134217728 | bytes 2097152 | tf_op jit(solution)/shard_map/early_part/pallas_call | solution.py:208
  9.2 4.0 %collective-permute-done.1.refs_2_ = f32[192,128]{1,0:T(8,128)S(1)} collective-permute-done((f32[192,128]{1,0:T(8,128)S(1)}, f32[192,128]{1,0:T(8,128)S(1)}, u32[]{:S(2)}, u32[]{:S(2)}) %collective-permute-start.1) | collective-permute-done | bytes 98336 | tf_op jit(solution)/shard_map/ppermute | solution.py:194
  13.3 0.0 collective-permute-done.2.refs_3_
  13.3 0.0 copy-done.4
  13.3 1.9 %correlate.1 = (f32[64,128]{1,0:T(8,128)}, f32[64,128]{1,0:T(8,128)}, f32[2]{0:T(128)}) custom-call(f32[2]{0:T(128)S(1)} %copy-done.4, f32[256,768]{1,0:T(8,128)S(1)} %early_part.1.coarse_ref, f32[192,128]{1,0:T(8,128)S(1)} %pad_maximum_fusion.block.refs_0_, f32[192,128]{1,0:T(8,128)S(1)} %collective-permute-done.block.refs_1_, ...), custom_call_target="tpu_custom_call" | custom-call | tf_op jit(solution)/shard_map/correlate/pallas_call | solution.py:218
Async XLA Ops:
  0.6 4.7 %copy-start.2 = (bf16[4,64,256]{2,1,0:T(8,128)(2,1)S(1)}, bf16[4,64,256]{2,1,0:T(8,128)(2,1)}, u32[]{:S(2)}) copy-start(bf16[4,64,256]{2,1,0:T(8,128)(2,1)} %constant.11.clone.last.refs_7_) | copy-start | bytes 393220
  1.5 7.5 %collective-permute-start = (f32[192,128]{1,0:T(8,128)S(1)}, f32[192,128]{1,0:T(8,128)S(1)}, u32[]{:S(2)}, u32[]{:S(2)}) collective-permute-start(f32[192,128]{1,0:T(8,128)S(1)} %pad_maximum_fusion.block.refs_0_), channel_id=1, source_target_pairs={{0,12},{4,8},{8,0},{12,4},{1,5},{5,13},{9,1},{13,9},{2,14},{6,10},... | collective-permute-start | bytes 294920 | tf_op jit(solution)/shard_map/ppermute | solution.py:194
  1.8 11.4 %collective-permute-start.1 = (f32[192,128]{1,0:T(8,128)S(1)}, f32[192,128]{1,0:T(8,128)S(1)}, u32[]{:S(2)}, u32[]{:S(2)}) collective-permute-start(f32[192,128]{1,0:T(8,128)S(1)} %pad_maximum_fusion.block.refs_0_), channel_id=1, source_target_pairs={{0,8},{4,12},{8,4},{12,0},{1,13},{5,9},{9,5},{13,1},{2,10},{6,14},... | collective-permute-start | bytes 294920 | tf_op jit(solution)/shard_map/ppermute | solution.py:194
  5.3 7.9 %collective-permute-start.2 = (f32[192,128]{1,0:T(8,128)S(1)}, f32[192,128]{1,0:T(8,128)S(1)}, u32[]{:S(2)}, u32[]{:S(2)}) collective-permute-start(f32[192,128]{1,0:T(8,128)S(1)} %pad_maximum_fusion.block.refs_0_), channel_id=1, source_target_pairs={{0,4},{4,0},{8,12},{12,8},{1,9},{5,1},{9,13},{13,5},{2,6},{6,2},{1... | collective-permute-start | bytes 294920 | tf_op jit(solution)/shard_map/ppermute | solution.py:194
  5.3 1.0 %copy-start = (bf16[256,512]{1,0:T(8,128)(2,1)S(1)}, bf16[256,512]{1,0:T(8,128)(2,1)}, u32[]{:S(2)}) copy-start(bf16[256,512]{1,0:T(8,128)(2,1)} %constant.8.clone.first.refs_4_) | copy-start | bytes 786436
  6.3 0.9 %copy-start.1 = (bf16[2,256,256]{2,1,0:T(8,128)(2,1)S(1)}, bf16[2,256,256]{2,1,0:T(8,128)(2,1)}, u32[]{:S(2)}) copy-start(bf16[2,256,256]{2,1,0:T(8,128)(2,1)} %constant.10.clone.second.refs_6_) | copy-start | bytes 786436
  7.2 0.9 %copy-start.3 = (f32[2,128,128]{2,1,0:T(8,128)S(1)}, f32[2,128,128]{2,1,0:T(8,128)}, u32[]{:S(2)}) copy-start(f32[2,128,128]{2,1,0:T(8,128)} %constant.9.clone.twiddle.refs_5_) | copy-start | bytes 393220
  8.4 4.9 %copy-start.4 = (f32[2]{0:T(128)S(1)}, f32[2]{0:T(128)}, u32[]{:S(2)}) copy-start(f32[2]{0:T(128)} %skip_ref.1) | copy-start | bytes 28

commit v3 on v2

--- a/solution.py
+++ b/solution.py
@@ -1,4 +1,5 @@
 import functools
+import itertools
 import math
 
 import jax
@@ -47,7 +48,9 @@
 
 
 def product(left, right):
-    return dot(jnp.concatenate([left[0], left[0], left[1]], axis=1), jnp.concatenate([right[0], right[1], right[0]]))
+    rows = left[0].shape[0]
+    both = dot(jnp.concatenate(left), right[0])
+    return both[:rows] + both[rows:] + dot(left[0], right[1])
 
 
 def stage_rows(block, channels):
@@ -67,25 +70,30 @@
 
 
 def routes(groups, cores):
-    plans = [(tuple(range(groups)), tuple(range(1, groups)))]
+    plain = (tuple(range(groups)), tuple(range(1, groups)))
+    plans = [[plain], [plain]]
     if groups == 4:
-        plans = [((0, 2, 1, 3), (3, 1, 2)), ((0, 1, 3, 2), (1, 2, 3))]
+        early, swift = ((0, 1, 3, 2), (1, 2, 3)), ((0, 2, 1, 3), (3, 1, 2))
+        plans = [[swift, early], [early, swift]]
     steps = []
     for index in range(groups - 1):
         targets = []
-        for core in range(cores):
-            cycle, moves = plans[core % len(plans)]
-            ahead = {cycle[place]: cycle[(place + moves[index]) % groups] for place in range(groups)}
-            targets.append([ahead[device] for device in range(groups)])
+        for line in plans:
+            for core in range(cores):
+                cycle, moves = line[core % len(line)]
+                ahead = {cycle[place]: cycle[(place + moves[index]) % groups] for place in range(groups)}
+                targets.append([ahead[device] for device in range(groups)])
         steps.append(targets)
     return steps
 
 
 def sender(targets):
+    line = jnp.where(lax.axis_index("parts") + lax.axis_index("chan") == 0, 0, 1)
+    kind = line * lax.axis_size("sub") + lax.axis_index("sub")
     code = 0
-    for core, ahead in enumerate(targets):
+    for index, ahead in enumerate(targets):
         packed = sum(device << 4 * target for device, target in enumerate(ahead))
-        code = jnp.where(lax.axis_index("sub") == core, packed, code)
+        code = jnp.where(kind == index, packed, code)
     return lax.bitwise_and(lax.shift_right_logical(code, 4 * lax.axis_index("seq")), 15)
 
 
@@ -111,9 +119,7 @@
     cos, sin = twiddle[0], twiddle[1]
     last_rows = last[device]
 
-    def stage1(channel):
-        lanes = slice(3 * channel * LANES, 3 * (channel + 1) * LANES)
-        return coarse_ref[:, lanes] + dot(columns, data[:, lanes])
+    coarse = coarse_ref[...] + dot(columns, data)
 
     def turn_out(coarse):
         part = []
@@ -150,7 +156,7 @@
         both = dot(last_rows, value[0])
         return both[:height] + both[height:] + dot(last_rows[:height], value[1])
 
-    turned = [turn_out(stage1(channel)) for channel in range(channels)]
+    turned = [turn_out(coarse[:, 3 * channel * LANES : 3 * (channel + 1) * LANES]) for channel in range(channels)]
     spectra = [wide(value) for value in turned]
     mixed = [mix(value) for value in spectra]
     back = [wide(value) for value in mixed]
@@ -184,14 +190,16 @@
     length = cells * groups
     rows = length // LANES
     own = jnp.concatenate([dense(filter_taps), dense(signal), dense(grad_out)])
-    cores = lax.axis_size("sub")
+    chans, cores = lax.axis_size("chan"), lax.axis_size("sub")
     steps = routes(groups, cores)
     arrived = []
     for targets in reversed(steps):
         hops = []
-        for core, ahead in enumerate(targets):
-            hops += [(device * cores + core, target * cores + core) for device, target in enumerate(ahead)]
-        arrived.insert(0, lax.ppermute(own, ("seq", "sub"), hops))
+        for part, chan, core in itertools.product(range(lax.axis_size("parts")), range(chans), range(cores)):
+            ahead = targets[core if part + chan == 0 else cores + core]
+            for device, target in enumerate(ahead):
+                hops.append(tuple(((part * groups + seq) * chans + chan) * cores + core for seq in (device, target)))
+        arrived.insert(0, lax.ppermute(own, ("parts", "seq", "chan", "sub"), hops))
     tables = [jnp.asarray(table) for table in gathered_tables(length, groups)]
     whole = pl.BlockSpec(memory_space=pltpu.VMEM)
     scalar = pl.BlockSpec(memory_space=pltpu.SMEM)

time: 15.3 us -> 15.3 us (level)
  no operation moved by 1% of the time
where the time goes in v3:
time: 15.3 us; the launch traced here: 15.1 us
  waiting for transfers between devices  4.6 us (30%)
  starting transfers between devices  3.86 us (25%)
  local copies, waits for them, and re-layouts  2.82 us (18%)
  Pallas kernels  2.32 us (15%)
  other arithmetic  0.83 us (5%)
  between operations  0.67 us (4%)
    ppermute x3, waiting for transfers between devices, gathered_body(): arrived.insert(0, lax.ppermute(own, ('parts', 'seq', 'chan', 'sub'), hops))  4.6 us
    ppermute x3, starting transfers between devices, gathered_body(): arrived.insert(0, lax.ppermute(own, ('parts', 'seq', 'chan', 'sub'), hops))  3.86 us
    unnamed x10, local copies, waits for them, and re-layouts  2.82 us
    pallas_call x1, Pallas kernels, gathered_body(): pl.pallas_call(functools.partial(gathered_kernel, groups, channels, steps...  1.83 us
    concatenate x1, other arithmetic, gathered_body(): own = jnp.concatenate([dense(filter_taps), dense(signal), dense(grad_out)])  0.83 us
  transfers between devices with their start and end apart: 3, of which 2 were waited for; matrix products, arithmetic and copies ran while one was open for 0% of the time, Pallas kernels for 3%

profile of v3, /device:TPU:24, one launch (start us, length us, event | category | flops | bytes accessed | tf_op | source)
XLA Modules:
  0.0 15.1 jit_solution(4095571195589473720)
XLA Ops:
  0.6 0.0 copy-start.2
  0.6 0.8 %pad_maximum_fusion.block.refs_0_ = f32[192,128]{1,0:T(8,128)S(1)} fusion(f32[64,128]{1,0:T(8,128)} %bitcast.25, f32[64,128]{1,0:T(8,128)} %bitcast.26, f32[64,128]{1,0:T(8,128)} %bitcast.27), kind=kLoop, calls=%fused_computation | loop fusion | flops 49152 | bytes 196608 | tf_op jit(solution)/shard_map/concatenate | solution.py:192
  1.5 0.4 %collective-permute-start = (f32[192,128]{1,0:T(8,128)S(1)}, f32[192,128]{1,0:T(8,128)S(1)}, u32[]{:S(2)}, u32[]{:S(2)}) collective-permute-start(f32[192,128]{1,0:T(8,128)S(1)} %pad_maximum_fusion.block.refs_0_), channel_id=1, source_target_pairs={{0,12},{4,8},{8,0},{12,4},{1,5},{5,13},{9,1},{13,9},{2,6},{6,14},{... | collective-permute-start | bytes 294920 | tf_op jit(solution)/shard_map/ppermute | solution.py:202
  1.8 3.5 %collective-permute-start.1 = (f32[192,128]{1,0:T(8,128)S(1)}, f32[192,128]{1,0:T(8,128)S(1)}, u32[]{:S(2)}, u32[]{:S(2)}) collective-permute-start(f32[192,128]{1,0:T(8,128)S(1)} %pad_maximum_fusion.block.refs_0_), channel_id=1, source_target_pairs={{0,8},{4,12},{8,4},{12,0},{1,13},{5,9},{9,5},{13,1},{2,14},{6,10},... | collective-permute-start | bytes 294920 | tf_op jit(solution)/shard_map/ppermute | solution.py:202
  5.3 0.0 collective-permute-start.2
  5.3 0.0 copy-done.2
  5.3 0.0 copy-start
  5.3 0.9 %copy-done = bf16[256,512]{1,0:T(8,128)(2,1)S(1)} copy-done((bf16[256,512]{1,0:T(8,128)(2,1)S(1)}, bf16[256,512]{1,0:T(8,128)(2,1)}, u32[]{:S(2)}) %copy-start) | copy-done | bytes 262168
  6.3 0.0 copy-start.1
  6.3 0.9 %copy-done.1 = bf16[2,256,256]{2,1,0:T(8,128)(2,1)S(1)} copy-done((bf16[2,256,256]{2,1,0:T(8,128)(2,1)S(1)}, bf16[2,256,256]{2,1,0:T(8,128)(2,1)}, u32[]{:S(2)}) %copy-start.1) | copy-done | bytes 262168
  7.2 0.0 copy-start.3
  7.2 0.9 %copy-done.3 = f32[2,128,128]{2,1,0:T(8,128)S(1)} copy-done((f32[2,128,128]{2,1,0:T(8,128)S(1)}, f32[2,128,128]{2,1,0:T(8,128)}, u32[]{:S(2)}) %copy-start.3) | copy-done | bytes 131096
  8.1 0.2 %own_part.1.coarse_ref = f32[256,768]{1,0:T(8,128)S(1)} custom-call(f32[192,128]{1,0:T(8,128)S(1)} %pad_maximum_fusion.block.refs_0_, bf16[256,512]{1,0:T(8,128)(2,1)S(1)} %copy-done, f32[2,128,128]{2,1,0:T(8,128)S(1)} %copy-done.3, bf16[2,256,256]{2,1,0:T(8,128)(2,1)S(1)} %copy-done.1, bf16[4,64,256]{2,1,0:T(8,128)(2,1)S(1)} %copy-done.2), custom_call_target="tpu_custom_call" | custom-call | flops 134217728 | bytes 2097152 | tf_op jit(solution)/shard_map/own_part/pallas_call | solution.py:207
  8.4 0.0 copy-start.4
  8.4 0.6 %collective-permute-done.block.refs_1_ = f32[192,128]{1,0:T(8,128)S(1)} collective-permute-done((f32[192,128]{1,0:T(8,128)S(1)}, f32[192,128]{1,0:T(8,128)S(1)}, u32[]{:S(2)}, u32[]{:S(2)}) %collective-permute-start) | collective-permute-done | bytes 98336 | tf_op jit(solution)/shard_map/ppermute | solution.py:202
  9.0 0.2 %early_part.1.coarse_ref = f32[256,768]{1,0:T(8,128)S(1)} custom-call(f32[256,768]{1,0:T(8,128)S(1)} %own_part.1.coarse_ref, f32[192,128]{1,0:T(8,128)S(1)} %collective-permute-done.block.refs_1_, bf16[256,512]{1,0:T(8,128)(2,1)S(1)} %copy-done), custom_call_target="tpu_custom_call" | custom-call | flops 134217728 | bytes 2097152 | tf_op jit(solution)/shard_map/early_part/pallas_call | solution.py:216
  9.2 4.0 %collective-permute-done.1.refs_2_ = f32[192,128]{1,0:T(8,128)S(1)} collective-permute-done((f32[192,128]{1,0:T(8,128)S(1)}, f32[192,128]{1,0:T(8,128)S(1)}, u32[]{:S(2)}, u32[]{:S(2)}) %collective-permute-start.1) | collective-permute-done | bytes 98336 | tf_op jit(solution)/shard_map/ppermute | solution.py:202
  13.3 0.0 collective-permute-done.2.refs_3_
  13.3 0.0 copy-done.4
  13.3 1.8 %correlate.1 = (f32[64,128]{1,0:T(8,128)}, f32[64,128]{1,0:T(8,128)}, f32[2]{0:T(128)}) custom-call(f32[2]{0:T(128)S(1)} %copy-done.4, f32[256,768]{1,0:T(8,128)S(1)} %early_part.1.coarse_ref, f32[192,128]{1,0:T(8,128)S(1)} %pad_maximum_fusion.block.refs_0_, f32[192,128]{1,0:T(8,128)S(1)} %collective-permute-done.block.refs_1_, ...), custom_call_target="tpu_custom_call" | custom-call | tf_op jit(solution)/shard_map/correlate/pallas_call | solution.py:226
Async XLA Ops:
  0.6 4.7 %copy-start.2 = (bf16[4,64,256]{2,1,0:T(8,128)(2,1)S(1)}, bf16[4,64,256]{2,1,0:T(8,128)(2,1)}, u32[]{:S(2)}) copy-start(bf16[4,64,256]{2,1,0:T(8,128)(2,1)} %constant.11.clone.last.refs_7_) | copy-start | bytes 393220
  1.5 7.5 %collective-permute-start = (f32[192,128]{1,0:T(8,128)S(1)}, f32[192,128]{1,0:T(8,128)S(1)}, u32[]{:S(2)}, u32[]{:S(2)}) collective-permute-start(f32[192,128]{1,0:T(8,128)S(1)} %pad_maximum_fusion.block.refs_0_), channel_id=1, source_target_pairs={{0,12},{4,8},{8,0},{12,4},{1,5},{5,13},{9,1},{13,9},{2,6},{6,14},{... | collective-permute-start | bytes 294920 | tf_op jit(solution)/shard_map/ppermute | solution.py:202
  1.8 11.4 %collective-permute-start.1 = (f32[192,128]{1,0:T(8,128)S(1)}, f32[192,128]{1,0:T(8,128)S(1)}, u32[]{:S(2)}, u32[]{:S(2)}) collective-permute-start(f32[192,128]{1,0:T(8,128)S(1)} %pad_maximum_fusion.block.refs_0_), channel_id=1, source_target_pairs={{0,8},{4,12},{8,4},{12,0},{1,13},{5,9},{9,5},{13,1},{2,14},{6,10},... | collective-permute-start | bytes 294920 | tf_op jit(solution)/shard_map/ppermute | solution.py:202
  5.3 7.9 %collective-permute-start.2 = (f32[192,128]{1,0:T(8,128)S(1)}, f32[192,128]{1,0:T(8,128)S(1)}, u32[]{:S(2)}, u32[]{:S(2)}) collective-permute-start(f32[192,128]{1,0:T(8,128)S(1)} %pad_maximum_fusion.block.refs_0_), channel_id=1, source_target_pairs={{0,4},{4,0},{8,12},{12,8},{1,9},{5,1},{9,13},{13,5},{2,10},{6,2},{... | collective-permute-start | bytes 294920 | tf_op jit(solution)/shard_map/ppermute | solution.py:202
  5.3 1.0 %copy-start = (bf16[256,512]{1,0:T(8,128)(2,1)S(1)}, bf16[256,512]{1,0:T(8,128)(2,1)}, u32[]{:S(2)}) copy-start(bf16[256,512]{1,0:T(8,128)(2,1)} %constant.8.clone.first.refs_4_) | copy-start | bytes 786436
  6.3 0.9 %copy-start.1 = (bf16[2,256,256]{2,1,0:T(8,128)(2,1)S(1)}, bf16[2,256,256]{2,1,0:T(8,128)(2,1)}, u32[]{:S(2)}) copy-start(bf16[2,256,256]{2,1,0:T(8,128)(2,1)} %constant.10.clone.second.refs_6_) | copy-start | bytes 786436
  7.2 0.9 %copy-start.3 = (f32[2,128,128]{2,1,0:T(8,128)S(1)}, f32[2,128,128]{2,1,0:T(8,128)}, u32[]{:S(2)}) copy-start(f32[2,128,128]{2,1,0:T(8,128)} %constant.9.clone.twiddle.refs_5_) | copy-start | bytes 393220
  8.4 4.9 %copy-start.4 = (f32[2]{0:T(128)S(1)}, f32[2]{0:T(128)}, u32[]{:S(2)}) copy-start(f32[2]{0:T(128)} %skip_ref.1) | copy-start | bytes 28

commit v4 on v2

--- a/solution.py
+++ b/solution.py
@@ -47,7 +47,9 @@
 
 
 def product(left, right):
-    return dot(jnp.concatenate([left[0], left[0], left[1]], axis=1), jnp.concatenate([right[0], right[1], right[0]]))
+    rows = left[0].shape[0]
+    both = dot(jnp.concatenate(left), right[0])
+    return both[:rows] + both[rows:] + dot(left[0], right[1])
 
 
 def stage_rows(block, channels):
@@ -111,9 +113,7 @@
     cos, sin = twiddle[0], twiddle[1]
     last_rows = last[device]
 
-    def stage1(channel):
-        lanes = slice(3 * channel * LANES, 3 * (channel + 1) * LANES)
-        return coarse_ref[:, lanes] + dot(columns, data[:, lanes])
+    coarse = coarse_ref[...] + dot(columns, data)
 
     def turn_out(coarse):
         part = []
@@ -150,7 +150,7 @@
         both = dot(last_rows, value[0])
         return both[:height] + both[height:] + dot(last_rows[:height], value[1])
 
-    turned = [turn_out(stage1(channel)) for channel in range(channels)]
+    turned = [turn_out(coarse[:, 3 * channel * LANES : 3 * (channel + 1) * LANES]) for channel in range(channels)]
     spectra = [wide(value) for value in turned]
     mixed = [mix(value) for value in spectra]
     back = [wide(value) for value in mixed]

time: 15.3 us -> 15.3 us (level)
  no operation moved by 1% of the time
where the time goes in v4:
time: 15.3 us; the launch traced here: 15.1 us
  waiting for transfers between devices  4.61 us (30%)
  starting transfers between devices  3.86 us (25%)
  local copies, waits for them, and re-layouts  2.82 us (18%)
  Pallas kernels  2.32 us (15%)
  other arithmetic  0.83 us (5%)
  between operations  0.67 us (4%)
    ppermute x3, waiting for transfers between devices, gathered_body(): arrived.insert(0, lax.ppermute(own, ('seq', 'sub'), hops))  4.61 us
    ppermute x3, starting transfers between devices, gathered_body(): arrived.insert(0, lax.ppermute(own, ('seq', 'sub'), hops))  3.86 us
    unnamed x10, local copies, waits for them, and re-layouts  2.82 us
    pallas_call x1, Pallas kernels, gathered_body(): pl.pallas_call(functools.partial(gathered_kernel, groups, channels, steps...  1.83 us
    concatenate x1, other arithmetic, gathered_body(): own = jnp.concatenate([dense(filter_taps), dense(signal), dense(grad_out)])  0.83 us
  transfers between devices with their start and end apart: 3, of which 2 were waited for; matrix products, arithmetic and copies ran while one was open for 0% of the time, Pallas kernels for 3%

profile of v4, /device:TPU:24, one launch (start us, length us, event | category | flops | bytes accessed | tf_op | source)
XLA Modules:
  0.0 15.1 jit_solution(5693413650141041109)
XLA Ops:
  0.6 0.0 copy-start.2
  0.6 0.8 %pad_maximum_fusion.block.refs_0_ = f32[192,128]{1,0:T(8,128)S(1)} fusion(f32[64,128]{1,0:T(8,128)} %bitcast.25, f32[64,128]{1,0:T(8,128)} %bitcast.26, f32[64,128]{1,0:T(8,128)} %bitcast.27), kind=kLoop, calls=%fused_computation | loop fusion | flops 49152 | bytes 196608 | tf_op jit(solution)/shard_map/concatenate | solution.py:186
  1.5 0.4 %collective-permute-start = (f32[192,128]{1,0:T(8,128)S(1)}, f32[192,128]{1,0:T(8,128)S(1)}, u32[]{:S(2)}, u32[]{:S(2)}) collective-permute-start(f32[192,128]{1,0:T(8,128)S(1)} %pad_maximum_fusion.block.refs_0_), channel_id=1, source_target_pairs={{0,12},{4,8},{8,0},{12,4},{1,5},{5,13},{9,1},{13,9},{2,14},{6,10},... | collective-permute-start | bytes 294920 | tf_op jit(solution)/shard_map/ppermute | solution.py:194
  1.8 3.5 %collective-permute-start.1 = (f32[192,128]{1,0:T(8,128)S(1)}, f32[192,128]{1,0:T(8,128)S(1)}, u32[]{:S(2)}, u32[]{:S(2)}) collective-permute-start(f32[192,128]{1,0:T(8,128)S(1)} %pad_maximum_fusion.block.refs_0_), channel_id=1, source_target_pairs={{0,8},{4,12},{8,4},{12,0},{1,13},{5,9},{9,5},{13,1},{2,10},{6,14},... | collective-permute-start | bytes 294920 | tf_op jit(solution)/shard_map/ppermute | solution.py:194
  5.3 0.0 collective-permute-start.2
  5.3 0.0 copy-done.2
  5.3 0.0 copy-start
  5.3 0.9 %copy-done = bf16[256,512]{1,0:T(8,128)(2,1)S(1)} copy-done((bf16[256,512]{1,0:T(8,128)(2,1)S(1)}, bf16[256,512]{1,0:T(8,128)(2,1)}, u32[]{:S(2)}) %copy-start) | copy-done | bytes 262168
  6.3 0.0 copy-start.1
  6.3 0.9 %copy-done.1 = bf16[2,256,256]{2,1,0:T(8,128)(2,1)S(1)} copy-done((bf16[2,256,256]{2,1,0:T(8,128)(2,1)S(1)}, bf16[2,256,256]{2,1,0:T(8,128)(2,1)}, u32[]{:S(2)}) %copy-start.1) | copy-done | bytes 262168
  7.2 0.0 copy-start.3
  7.2 0.9 %copy-done.3 = f32[2,128,128]{2,1,0:T(8,128)S(1)} copy-done((f32[2,128,128]{2,1,0:T(8,128)S(1)}, f32[2,128,128]{2,1,0:T(8,128)}, u32[]{:S(2)}) %copy-start.3) | copy-done | bytes 131096
  8.1 0.2 %own_part.1.coarse_ref = f32[256,768]{1,0:T(8,128)S(1)} custom-call(f32[192,128]{1,0:T(8,128)S(1)} %pad_maximum_fusion.block.refs_0_, bf16[256,512]{1,0:T(8,128)(2,1)S(1)} %copy-done, f32[2,128,128]{2,1,0:T(8,128)S(1)} %copy-done.3, bf16[2,256,256]{2,1,0:T(8,128)(2,1)S(1)} %copy-done.1, bf16[4,64,256]{2,1,0:T(8,128)(2,1)S(1)} %copy-done.2), custom_call_target="tpu_custom_call" | custom-call | flops 134217728 | bytes 2097152 | tf_op jit(solution)/shard_map/own_part/pallas_call | solution.py:199
  8.4 0.0 copy-start.4
  8.4 0.6 %collective-permute-done.block.refs_1_ = f32[192,128]{1,0:T(8,128)S(1)} collective-permute-done((f32[192,128]{1,0:T(8,128)S(1)}, f32[192,128]{1,0:T(8,128)S(1)}, u32[]{:S(2)}, u32[]{:S(2)}) %collective-permute-start) | collective-permute-done | bytes 98336 | tf_op jit(solution)/shard_map/ppermute | solution.py:194
  9.0 0.2 %early_part.1.coarse_ref = f32[256,768]{1,0:T(8,128)S(1)} custom-call(f32[256,768]{1,0:T(8,128)S(1)} %own_part.1.coarse_ref, f32[192,128]{1,0:T(8,128)S(1)} %collective-permute-done.block.refs_1_, bf16[256,512]{1,0:T(8,128)(2,1)S(1)} %copy-done), custom_call_target="tpu_custom_call" | custom-call | flops 134217728 | bytes 2097152 | tf_op jit(solution)/shard_map/early_part/pallas_call | solution.py:208
  9.2 4.0 %collective-permute-done.1.refs_2_ = f32[192,128]{1,0:T(8,128)S(1)} collective-permute-done((f32[192,128]{1,0:T(8,128)S(1)}, f32[192,128]{1,0:T(8,128)S(1)}, u32[]{:S(2)}, u32[]{:S(2)}) %collective-permute-start.1) | collective-permute-done | bytes 98336 | tf_op jit(solution)/shard_map/ppermute | solution.py:194
  13.3 0.0 collective-permute-done.2.refs_3_
  13.3 0.0 copy-done.4
  13.3 1.8 %correlate.1 = (f32[64,128]{1,0:T(8,128)}, f32[64,128]{1,0:T(8,128)}, f32[2]{0:T(128)}) custom-call(f32[2]{0:T(128)S(1)} %copy-done.4, f32[256,768]{1,0:T(8,128)S(1)} %early_part.1.coarse_ref, f32[192,128]{1,0:T(8,128)S(1)} %pad_maximum_fusion.block.refs_0_, f32[192,128]{1,0:T(8,128)S(1)} %collective-permute-done.block.refs_1_, ...), custom_call_target="tpu_custom_call" | custom-call | tf_op jit(solution)/shard_map/correlate/pallas_call | solution.py:218
Async XLA Ops:
  0.6 4.7 %copy-start.2 = (bf16[4,64,256]{2,1,0:T(8,128)(2,1)S(1)}, bf16[4,64,256]{2,1,0:T(8,128)(2,1)}, u32[]{:S(2)}) copy-start(bf16[4,64,256]{2,1,0:T(8,128)(2,1)} %constant.11.clone.last.refs_7_) | copy-start | bytes 393220
  1.5 7.5 %collective-permute-start = (f32[192,128]{1,0:T(8,128)S(1)}, f32[192,128]{1,0:T(8,128)S(1)}, u32[]{:S(2)}, u32[]{:S(2)}) collective-permute-start(f32[192,128]{1,0:T(8,128)S(1)} %pad_maximum_fusion.block.refs_0_), channel_id=1, source_target_pairs={{0,12},{4,8},{8,0},{12,4},{1,5},{5,13},{9,1},{13,9},{2,14},{6,10},... | collective-permute-start | bytes 294920 | tf_op jit(solution)/shard_map/ppermute | solution.py:194
  1.8 11.4 %collective-permute-start.1 = (f32[192,128]{1,0:T(8,128)S(1)}, f32[192,128]{1,0:T(8,128)S(1)}, u32[]{:S(2)}, u32[]{:S(2)}) collective-permute-start(f32[192,128]{1,0:T(8,128)S(1)} %pad_maximum_fusion.block.refs_0_), channel_id=1, source_target_pairs={{0,8},{4,12},{8,4},{12,0},{1,13},{5,9},{9,5},{13,1},{2,10},{6,14},... | collective-permute-start | bytes 294920 | tf_op jit(solution)/shard_map/ppermute | solution.py:194
  5.3 7.9 %collective-permute-start.2 = (f32[192,128]{1,0:T(8,128)S(1)}, f32[192,128]{1,0:T(8,128)S(1)}, u32[]{:S(2)}, u32[]{:S(2)}) collective-permute-start(f32[192,128]{1,0:T(8,128)S(1)} %pad_maximum_fusion.block.refs_0_), channel_id=1, source_target_pairs={{0,4},{4,0},{8,12},{12,8},{1,9},{5,1},{9,13},{13,5},{2,6},{6,2},{1... | collective-permute-start | bytes 294920 | tf_op jit(solution)/shard_map/ppermute | solution.py:194
  5.3 1.0 %copy-start = (bf16[256,512]{1,0:T(8,128)(2,1)S(1)}, bf16[256,512]{1,0:T(8,128)(2,1)}, u32[]{:S(2)}) copy-start(bf16[256,512]{1,0:T(8,128)(2,1)} %constant.8.clone.first.refs_4_) | copy-start | bytes 786436
  6.3 0.9 %copy-start.1 = (bf16[2,256,256]{2,1,0:T(8,128)(2,1)S(1)}, bf16[2,256,256]{2,1,0:T(8,128)(2,1)}, u32[]{:S(2)}) copy-start(bf16[2,256,256]{2,1,0:T(8,128)(2,1)} %constant.10.clone.second.refs_6_) | copy-start | bytes 786436
  7.2 0.9 %copy-start.3 = (f32[2,128,128]{2,1,0:T(8,128)S(1)}, f32[2,128,128]{2,1,0:T(8,128)}, u32[]{:S(2)}) copy-start(f32[2,128,128]{2,1,0:T(8,128)} %constant.9.clone.twiddle.refs_5_) | copy-start | bytes 393220
  8.4 4.9 %copy-start.4 = (f32[2]{0:T(128)S(1)}, f32[2]{0:T(128)}, u32[]{:S(2)}) copy-start(f32[2]{0:T(128)} %skip_ref.1) | copy-start | bytes 28

commit v5 on v4

--- a/solution.py
+++ b/solution.py
@@ -47,9 +47,7 @@
 
 
 def product(left, right):
-    rows = left[0].shape[0]
-    both = dot(jnp.concatenate(left), right[0])
-    return both[:rows] + both[rows:] + dot(left[0], right[1])
+    return dot(jnp.concatenate([left[0], left[0], left[1]], axis=1), jnp.concatenate([right[0], right[1], right[0]]))
 
 
 def stage_rows(block, channels):
@@ -93,10 +91,6 @@
 
 def own_kernel(channels, block, first, twiddle, second, last, out_ref):
     out_ref[...] = dot(stage_columns(first, lax.axis_index("seq")), stage_rows(block, channels))
-
-
-def early_kernel(channels, targets, coarse_ref, block, first, out_ref):
-    out_ref[...] = coarse_ref[...] + dot(stage_columns(first, sender(targets)), stage_rows(block, channels))
 
 
 def gathered_kernel(groups, channels, late, skip_ref, coarse_ref, *refs):
@@ -205,24 +199,15 @@
         cost_estimate=pl.CostEstimate(flops=2**27, bytes_accessed=2**21, transcendentals=0),
         name="own_part",
     )(own, *tables)
-    coarse = pl.pallas_call(
-        functools.partial(early_kernel, channels, steps[0]),
-        out_shape=jax.ShapeDtypeStruct(coarse.shape, jnp.float32),
-        in_specs=[whole] * 3,
-        out_specs=whole,
-        compiler_params=params,
-        cost_estimate=pl.CostEstimate(flops=2**27, bytes_accessed=2**21, transcendentals=0),
-        name="early_part",
-    )(coarse, arrived[0], tables[0])
     shape = jax.ShapeDtypeStruct(dense(signal).shape, jnp.float32)
     grad_signal, grad_filter, grad_skip = pl.pallas_call(
-        functools.partial(gathered_kernel, groups, channels, steps[1:]),
+        functools.partial(gathered_kernel, groups, channels, steps[::-1]),
         out_shape=(shape, shape, jax.ShapeDtypeStruct((channels,), jnp.float32)),
         in_specs=[whole] + [whole] * (groups + 5),
         out_specs=(whole, whole, scalar),
         compiler_params=params,
         name="correlate",
-    )(skip, coarse, own, *arrived, *tables)
+    )(skip, coarse, own, *arrived[::-1], *tables)
     return (undense(grad_signal, channels), undense(grad_filter, channels), grad_skip)
 
 

time: 15.3 us -> 15.4 us (level)
  waiting for transfers between devices: 4.61 us -> 4.87 us
  Pallas kernels: 2.32 us -> 2.16 us
    ppermute x3, waiting for transfers between devices: 4.61 us -> 4.87 us  [gathered_body(): arrived.insert(0, lax.ppermute(own, ('seq', 'sub'), hops))]
    pallas_call x1 -> x0, Pallas kernels: 0.25 us -> none  [gathered_body(): pl.pallas_call(functools.partial(early_kernel, channels, steps[0]), out_s...]
  transfers between devices with their start and end apart: 3 -> 3, of which waited for: 2 -> 2; matrix products, arithmetic and copies ran while one was open for 0% -> 0% of each run, Pallas kernels for 3% -> 2%
where the time goes in v5:
time: 15.4 us; the launch traced here: 15.2 us
  waiting for transfers between devices  4.87 us (32%)
  starting transfers between devices  3.86 us (25%)
  local copies, waits for them, and re-layouts  2.81 us (18%)
  Pallas kernels  2.16 us (14%)
  other arithmetic  0.83 us (5%)
  between operations  0.66 us (4%)
    ppermute x3, waiting for transfers between devices, gathered_body(): arrived.insert(0, lax.ppermute(own, ('seq', 'sub'), hops))  4.87 us
    ppermute x3, starting transfers between devices, gathered_body(): arrived.insert(0, lax.ppermute(own, ('seq', 'sub'), hops))  3.86 us
    unnamed x10, local copies, waits for them, and re-layouts  2.81 us
    pallas_call x1, Pallas kernels, gathered_body(): pl.pallas_call(functools.partial(gathered_kernel, groups, channels, steps...  1.91 us
    concatenate x1, other arithmetic, gathered_body(): own = jnp.concatenate([dense(filter_taps), dense(signal), dense(grad_out)])  0.83 us
  transfers between devices with their start and end apart: 3, of which 2 were waited for; matrix products, arithmetic and copies ran while one was open for 0% of the time, Pallas kernels for 2%

profile of v5, /device:TPU:24, one launch (start us, length us, event | category | flops | bytes accessed | tf_op | source)
XLA Modules:
  0.0 15.2 jit_solution(8195366566650723136)
XLA Ops:
  0.6 0.0 copy-start.2
  0.6 0.0 copy-start.4
  0.7 0.8 %pad_maximum_fusion.block.refs_0_ = f32[192,128]{1,0:T(8,128)S(1)} fusion(f32[64,128]{1,0:T(8,128)} %bitcast.25, f32[64,128]{1,0:T(8,128)} %bitcast.26, f32[64,128]{1,0:T(8,128)} %bitcast.27), kind=kLoop, calls=%fused_computation | loop fusion | flops 49152 | bytes 196608 | tf_op jit(solution)/shard_map/concatenate | solution.py:180
  1.5 0.4 %collective-permute-start.2 = (f32[192,128]{1,0:T(8,128)S(1)}, f32[192,128]{1,0:T(8,128)S(1)}, u32[]{:S(2)}, u32[]{:S(2)}) collective-permute-start(f32[192,128]{1,0:T(8,128)S(1)} %pad_maximum_fusion.block.refs_0_), channel_id=1, source_target_pairs={{0,12},{4,8},{8,0},{12,4},{1,5},{5,13},{9,1},{13,9},{2,14},{6,10},... | collective-permute-start | bytes 294920 | tf_op jit(solution)/shard_map/ppermute | solution.py:188
  1.9 3.5 %collective-permute-start.1 = (f32[192,128]{1,0:T(8,128)S(1)}, f32[192,128]{1,0:T(8,128)S(1)}, u32[]{:S(2)}, u32[]{:S(2)}) collective-permute-start(f32[192,128]{1,0:T(8,128)S(1)} %pad_maximum_fusion.block.refs_0_), channel_id=1, source_target_pairs={{0,8},{4,12},{8,4},{12,0},{1,13},{5,9},{9,5},{13,1},{2,10},{6,14},... | collective-permute-start | bytes 294920 | tf_op jit(solution)/shard_map/ppermute | solution.py:188
  5.3 0.0 collective-permute-start
  5.3 0.0 copy-done.2
  5.3 0.0 copy-start
  5.3 0.9 %copy-done = bf16[2,256,256]{2,1,0:T(8,128)(2,1)S(1)} copy-done((bf16[2,256,256]{2,1,0:T(8,128)(2,1)S(1)}, bf16[2,256,256]{2,1,0:T(8,128)(2,1)}, u32[]{:S(2)}) %copy-start) | copy-done | bytes 262168
  6.3 0.0 copy-start.1
  6.3 0.9 %copy-done.1 = bf16[256,512]{1,0:T(8,128)(2,1)S(1)} copy-done((bf16[256,512]{1,0:T(8,128)(2,1)S(1)}, bf16[256,512]{1,0:T(8,128)(2,1)}, u32[]{:S(2)}) %copy-start.1) | copy-done | bytes 262168
  7.2 0.0 copy-start.3
  7.3 0.9 %copy-done.3 = f32[2,128,128]{2,1,0:T(8,128)S(1)} copy-done((f32[2,128,128]{2,1,0:T(8,128)S(1)}, f32[2,128,128]{2,1,0:T(8,128)}, u32[]{:S(2)}) %copy-start.3) | copy-done | bytes 131096
  8.2 0.2 %own_part.1.coarse_ref = f32[256,768]{1,0:T(8,128)S(1)} custom-call(f32[192,128]{1,0:T(8,128)S(1)} %pad_maximum_fusion.block.refs_0_, bf16[256,512]{1,0:T(8,128)(2,1)S(1)} %copy-done.1, f32[2,128,128]{2,1,0:T(8,128)S(1)} %copy-done.3, bf16[2,256,256]{2,1,0:T(8,128)(2,1)S(1)} %copy-done, bf16[4,64,256]{2,1,0:T(8,128)(2,1)S(1)} %copy-done.2), custom_call_target="tpu_custom_call" | custom-call | flops 134217728 | bytes 2097152 | tf_op jit(solution)/shard_map/own_part/pallas_call | solution.py:193
  8.4 0.6 %collective-permute-done.2.refs_3_ = f32[192,128]{1,0:T(8,128)S(1)} collective-permute-done((f32[192,128]{1,0:T(8,128)S(1)}, f32[192,128]{1,0:T(8,128)S(1)}, u32[]{:S(2)}, u32[]{:S(2)}) %collective-permute-start.2) | collective-permute-done | bytes 98336 | tf_op jit(solution)/shard_map/ppermute | solution.py:188
  9.0 4.3 %collective-permute-done.1.refs_2_ = f32[192,128]{1,0:T(8,128)S(1)} collective-permute-done((f32[192,128]{1,0:T(8,128)S(1)}, f32[192,128]{1,0:T(8,128)S(1)}, u32[]{:S(2)}, u32[]{:S(2)}) %collective-permute-start.1) | collective-permute-done | bytes 98336 | tf_op jit(solution)/shard_map/ppermute | solution.py:188
  13.3 0.0 collective-permute-done.refs_1_
  13.3 0.0 copy-done.4
  13.3 1.9 %correlate.1 = (f32[64,128]{1,0:T(8,128)}, f32[64,128]{1,0:T(8,128)}, f32[2]{0:T(128)}) custom-call(f32[2]{0:T(128)S(1)} %copy-done.4, f32[256,768]{1,0:T(8,128)S(1)} %own_part.1.coarse_ref, f32[192,128]{1,0:T(8,128)S(1)} %pad_maximum_fusion.block.refs_0_, f32[192,128]{1,0:T(8,128)S(1)} %collective-permute-done.refs_1_, ...), custom_call_target="tpu_custom_call" | custom-call | tf_op jit(solution)/shard_map/correlate/pallas_call | solution.py:203
Async XLA Ops:
  0.6 4.7 %copy-start.2 = (bf16[4,64,256]{2,1,0:T(8,128)(2,1)S(1)}, bf16[4,64,256]{2,1,0:T(8,128)(2,1)}, u32[]{:S(2)}) copy-start(bf16[4,64,256]{2,1,0:T(8,128)(2,1)} %constant.11.clone.last.refs_7_) | copy-start | bytes 393220
  0.6 12.6 %copy-start.4 = (f32[2]{0:T(128)S(1)}, f32[2]{0:T(128)}, u32[]{:S(2)}) copy-start(f32[2]{0:T(128)} %skip_ref.1) | copy-start | bytes 28
  1.5 7.5 %collective-permute-start.2 = (f32[192,128]{1,0:T(8,128)S(1)}, f32[192,128]{1,0:T(8,128)S(1)}, u32[]{:S(2)}, u32[]{:S(2)}) collective-permute-start(f32[192,128]{1,0:T(8,128)S(1)} %pad_maximum_fusion.block.refs_0_), channel_id=1, source_target_pairs={{0,12},{4,8},{8,0},{12,4},{1,5},{5,13},{9,1},{13,9},{2,14},{6,10},... | collective-permute-start | bytes 294920 | tf_op jit(solution)/shard_map/ppermute | solution.py:188
  1.9 11.4 %collective-permute-start.1 = (f32[192,128]{1,0:T(8,128)S(1)}, f32[192,128]{1,0:T(8,128)S(1)}, u32[]{:S(2)}, u32[]{:S(2)}) collective-permute-start(f32[192,128]{1,0:T(8,128)S(1)} %pad_maximum_fusion.block.refs_0_), channel_id=1, source_target_pairs={{0,8},{4,12},{8,4},{12,0},{1,13},{5,9},{9,5},{13,1},{2,10},{6,14},... | collective-permute-start | bytes 294920 | tf_op jit(solution)/shard_map/ppermute | solution.py:188
  5.3 7.9 %collective-permute-start = (f32[192,128]{1,0:T(8,128)S(1)}, f32[192,128]{1,0:T(8,128)S(1)}, u32[]{:S(2)}, u32[]{:S(2)}) collective-permute-start(f32[192,128]{1,0:T(8,128)S(1)} %pad_maximum_fusion.block.refs_0_), channel_id=1, source_target_pairs={{0,4},{4,0},{8,12},{12,8},{1,9},{5,1},{9,13},{13,5},{2,6},{6,2},{1... | collective-permute-start | bytes 294920 | tf_op jit(solution)/shard_map/ppermute | solution.py:188
  5.3 1.0 %copy-start = (bf16[2,256,256]{2,1,0:T(8,128)(2,1)S(1)}, bf16[2,256,256]{2,1,0:T(8,128)(2,1)}, u32[]{:S(2)}) copy-start(bf16[2,256,256]{2,1,0:T(8,128)(2,1)} %constant.10.clone.second.refs_6_) | copy-start | bytes 786436
  6.3 0.9 %copy-start.1 = (bf16[256,512]{1,0:T(8,128)(2,1)S(1)}, bf16[256,512]{1,0:T(8,128)(2,1)}, u32[]{:S(2)}) copy-start(bf16[256,512]{1,0:T(8,128)(2,1)} %constant.8.clone.first.refs_4_) | copy-start | bytes 786436
  7.2 0.9 %copy-start.3 = (f32[2,128,128]{2,1,0:T(8,128)S(1)}, f32[2,128,128]{2,1,0:T(8,128)}, u32[]{:S(2)}) copy-start(f32[2,128,128]{2,1,0:T(8,128)} %constant.9.clone.twiddle.refs_5_) | copy-start | bytes 393220

commit v6 on v4

--- a/solution.py
+++ b/solution.py
@@ -47,9 +47,7 @@
 
 
 def product(left, right):
-    rows = left[0].shape[0]
-    both = dot(jnp.concatenate(left), right[0])
-    return both[:rows] + both[rows:] + dot(left[0], right[1])
+    return dot(jnp.concatenate([left[0], left[0], left[1]], axis=1), jnp.concatenate([right[0], right[1], right[0]]))
 
 
 def stage_rows(block, channels):

time: 15.3 us -> 15.3 us (level)
  no operation moved by 1% of the time
where the time goes in v6:
time: 15.3 us; the launch traced here: 15.1 us
  waiting for transfers between devices  4.61 us (30%)
  starting transfers between devices  3.86 us (25%)
  local copies, waits for them, and re-layouts  2.82 us (18%)
  Pallas kernels  2.32 us (15%)
  other arithmetic  0.83 us (5%)
  between operations  0.67 us (4%)
    ppermute x3, waiting for transfers between devices, gathered_body(): arrived.insert(0, lax.ppermute(own, ('seq', 'sub'), hops))  4.61 us
    ppermute x3, starting transfers between devices, gathered_body(): arrived.insert(0, lax.ppermute(own, ('seq', 'sub'), hops))  3.86 us
    unnamed x10, local copies, waits for them, and re-layouts  2.82 us
    pallas_call x1, Pallas kernels, gathered_body(): pl.pallas_call(functools.partial(gathered_kernel, groups, channels, steps...  1.83 us
    concatenate x1, other arithmetic, gathered_body(): own = jnp.concatenate([dense(filter_taps), dense(signal), dense(grad_out)])  0.83 us
  transfers between devices with their start and end apart: 3, of which 2 were waited for; matrix products, arithmetic and copies ran while one was open for 0% of the time, Pallas kernels for 3%

profile of v6, /device:TPU:24, one launch (start us, length us, event | category | flops | bytes accessed | tf_op | source)
XLA Modules:
  0.0 15.1 jit_solution(6959481883420700849)
XLA Ops:
  0.6 0.0 copy-start.2
  0.6 0.8 %pad_maximum_fusion.block.refs_0_ = f32[192,128]{1,0:T(8,128)S(1)} fusion(f32[64,128]{1,0:T(8,128)} %bitcast.25, f32[64,128]{1,0:T(8,128)} %bitcast.26, f32[64,128]{1,0:T(8,128)} %bitcast.27), kind=kLoop, calls=%fused_computation | loop fusion | flops 49152 | bytes 196608 | tf_op jit(solution)/shard_map/concatenate | solution.py:184
  1.5 0.4 %collective-permute-start = (f32[192,128]{1,0:T(8,128)S(1)}, f32[192,128]{1,0:T(8,128)S(1)}, u32[]{:S(2)}, u32[]{:S(2)}) collective-permute-start(f32[192,128]{1,0:T(8,128)S(1)} %pad_maximum_fusion.block.refs_0_), channel_id=1, source_target_pairs={{0,12},{4,8},{8,0},{12,4},{1,5},{5,13},{9,1},{13,9},{2,14},{6,10},... | collective-permute-start | bytes 294920 | tf_op jit(solution)/shard_map/ppermute | solution.py:192
  1.8 3.5 %collective-permute-start.1 = (f32[192,128]{1,0:T(8,128)S(1)}, f32[192,128]{1,0:T(8,128)S(1)}, u32[]{:S(2)}, u32[]{:S(2)}) collective-permute-start(f32[192,128]{1,0:T(8,128)S(1)} %pad_maximum_fusion.block.refs_0_), channel_id=1, source_target_pairs={{0,8},{4,12},{8,4},{12,0},{1,13},{5,9},{9,5},{13,1},{2,10},{6,14},... | collective-permute-start | bytes 294920 | tf_op jit(solution)/shard_map/ppermute | solution.py:192
  5.3 0.0 collective-permute-start.2
  5.3 0.0 copy-done.2
  5.3 0.0 copy-start
  5.3 0.9 %copy-done = bf16[256,512]{1,0:T(8,128)(2,1)S(1)} copy-done((bf16[256,512]{1,0:T(8,128)(2,1)S(1)}, bf16[256,512]{1,0:T(8,128)(2,1)}, u32[]{:S(2)}) %copy-start) | copy-done | bytes 262168
  6.3 0.0 copy-start.1
  6.3 0.9 %copy-done.1 = bf16[2,256,256]{2,1,0:T(8,128)(2,1)S(1)} copy-done((bf16[2,256,256]{2,1,0:T(8,128)(2,1)S(1)}, bf16[2,256,256]{2,1,0:T(8,128)(2,1)}, u32[]{:S(2)}) %copy-start.1) | copy-done | bytes 262168
  7.2 0.0 copy-start.3
  7.2 0.9 %copy-done.3 = f32[2,128,128]{2,1,0:T(8,128)S(1)} copy-done((f32[2,128,128]{2,1,0:T(8,128)S(1)}, f32[2,128,128]{2,1,0:T(8,128)}, u32[]{:S(2)}) %copy-start.3) | copy-done | bytes 131096
  8.1 0.2 %own_part.1.coarse_ref = f32[256,768]{1,0:T(8,128)S(1)} custom-call(f32[192,128]{1,0:T(8,128)S(1)} %pad_maximum_fusion.block.refs_0_, bf16[256,512]{1,0:T(8,128)(2,1)S(1)} %copy-done, f32[2,128,128]{2,1,0:T(8,128)S(1)} %copy-done.3, bf16[2,256,256]{2,1,0:T(8,128)(2,1)S(1)} %copy-done.1, bf16[4,64,256]{2,1,0:T(8,128)(2,1)S(1)} %copy-done.2), custom_call_target="tpu_custom_call" | custom-call | flops 134217728 | bytes 2097152 | tf_op jit(solution)/shard_map/own_part/pallas_call | solution.py:197
  8.4 0.0 copy-start.4
  8.4 0.6 %collective-permute-done.block.refs_1_ = f32[192,128]{1,0:T(8,128)S(1)} collective-permute-done((f32[192,128]{1,0:T(8,128)S(1)}, f32[192,128]{1,0:T(8,128)S(1)}, u32[]{:S(2)}, u32[]{:S(2)}) %collective-permute-start) | collective-permute-done | bytes 98336 | tf_op jit(solution)/shard_map/ppermute | solution.py:192
  9.0 0.2 %early_part.1.coarse_ref = f32[256,768]{1,0:T(8,128)S(1)} custom-call(f32[256,768]{1,0:T(8,128)S(1)} %own_part.1.coarse_ref, f32[192,128]{1,0:T(8,128)S(1)} %collective-permute-done.block.refs_1_, bf16[256,512]{1,0:T(8,128)(2,1)S(1)} %copy-done), custom_call_target="tpu_custom_call" | custom-call | flops 134217728 | bytes 2097152 | tf_op jit(solution)/shard_map/early_part/pallas_call | solution.py:206
  9.2 4.0 %collective-permute-done.1.refs_2_ = f32[192,128]{1,0:T(8,128)S(1)} collective-permute-done((f32[192,128]{1,0:T(8,128)S(1)}, f32[192,128]{1,0:T(8,128)S(1)}, u32[]{:S(2)}, u32[]{:S(2)}) %collective-permute-start.1) | collective-permute-done | bytes 98336 | tf_op jit(solution)/shard_map/ppermute | solution.py:192
  13.3 0.0 collective-permute-done.2.refs_3_
  13.3 0.0 copy-done.4
  13.3 1.8 %correlate.1 = (f32[64,128]{1,0:T(8,128)}, f32[64,128]{1,0:T(8,128)}, f32[2]{0:T(128)}) custom-call(f32[2]{0:T(128)S(1)} %copy-done.4, f32[256,768]{1,0:T(8,128)S(1)} %early_part.1.coarse_ref, f32[192,128]{1,0:T(8,128)S(1)} %pad_maximum_fusion.block.refs_0_, f32[192,128]{1,0:T(8,128)S(1)} %collective-permute-done.block.refs_1_, ...), custom_call_target="tpu_custom_call" | custom-call | tf_op jit(solution)/shard_map/correlate/pallas_call | solution.py:216
Async XLA Ops:
  0.6 4.7 %copy-start.2 = (bf16[4,64,256]{2,1,0:T(8,128)(2,1)S(1)}, bf16[4,64,256]{2,1,0:T(8,128)(2,1)}, u32[]{:S(2)}) copy-start(bf16[4,64,256]{2,1,0:T(8,128)(2,1)} %constant.11.clone.last.refs_7_) | copy-start | bytes 393220
  1.5 7.5 %collective-permute-start = (f32[192,128]{1,0:T(8,128)S(1)}, f32[192,128]{1,0:T(8,128)S(1)}, u32[]{:S(2)}, u32[]{:S(2)}) collective-permute-start(f32[192,128]{1,0:T(8,128)S(1)} %pad_maximum_fusion.block.refs_0_), channel_id=1, source_target_pairs={{0,12},{4,8},{8,0},{12,4},{1,5},{5,13},{9,1},{13,9},{2,14},{6,10},... | collective-permute-start | bytes 294920 | tf_op jit(solution)/shard_map/ppermute | solution.py:192
  1.8 11.4 %collective-permute-start.1 = (f32[192,128]{1,0:T(8,128)S(1)}, f32[192,128]{1,0:T(8,128)S(1)}, u32[]{:S(2)}, u32[]{:S(2)}) collective-permute-start(f32[192,128]{1,0:T(8,128)S(1)} %pad_maximum_fusion.block.refs_0_), channel_id=1, source_target_pairs={{0,8},{4,12},{8,4},{12,0},{1,13},{5,9},{9,5},{13,1},{2,10},{6,14},... | collective-permute-start | bytes 294920 | tf_op jit(solution)/shard_map/ppermute | solution.py:192
  5.3 7.9 %collective-permute-start.2 = (f32[192,128]{1,0:T(8,128)S(1)}, f32[192,128]{1,0:T(8,128)S(1)}, u32[]{:S(2)}, u32[]{:S(2)}) collective-permute-start(f32[192,128]{1,0:T(8,128)S(1)} %pad_maximum_fusion.block.refs_0_), channel_id=1, source_target_pairs={{0,4},{4,0},{8,12},{12,8},{1,9},{5,1},{9,13},{13,5},{2,6},{6,2},{1... | collective-permute-start | bytes 294920 | tf_op jit(solution)/shard_map/ppermute | solution.py:192
  5.3 1.0 %copy-start = (bf16[256,512]{1,0:T(8,128)(2,1)S(1)}, bf16[256,512]{1,0:T(8,128)(2,1)}, u32[]{:S(2)}) copy-start(bf16[256,512]{1,0:T(8,128)(2,1)} %constant.8.clone.first.refs_4_) | copy-start | bytes 786436
  6.3 0.9 %copy-start.1 = (bf16[2,256,256]{2,1,0:T(8,128)(2,1)S(1)}, bf16[2,256,256]{2,1,0:T(8,128)(2,1)}, u32[]{:S(2)}) copy-start(bf16[2,256,256]{2,1,0:T(8,128)(2,1)} %constant.10.clone.second.refs_6_) | copy-start | bytes 786436
  7.2 0.9 %copy-start.3 = (f32[2,128,128]{2,1,0:T(8,128)S(1)}, f32[2,128,128]{2,1,0:T(8,128)}, u32[]{:S(2)}) copy-start(f32[2,128,128]{2,1,0:T(8,128)} %constant.9.clone.twiddle.refs_5_) | copy-start | bytes 393220
  8.4 4.9 %copy-start.4 = (f32[2]{0:T(128)S(1)}, f32[2]{0:T(128)}, u32[]{:S(2)}) copy-start(f32[2]{0:T(128)} %skip_ref.1) | copy-start | bytes 28
